TPU v7x, 32 devices: a whole 2x2x4 slice. The times are simulated.
32 devices in a mesh: dp: 2 (over y), mp: 16 (over z, x, core).
Axes of the slice: x: 2, y: 2, z: 4, core: 2. Of those that a mesh axis runs over, the one named last changes fastest.
Arguments:
- tokens: bfloat16 [32, 1024, 1024], P(('dp', 'mp')), may hold values from -6 to 6
- segment_ids: int32 [32, 1024], P(('dp', 'mp')), may hold values from 0 to 15, never falling along the last dimension, each value on 1 to 128 neighbouring positions
- qkv_weight: bfloat16 [1024, 3072], replicated, may hold values from -0.1875 to 0.1875
- prefix_keys: bfloat16 [64, 1024], replicated, may hold values from -6 to 6
- prefix_values: bfloat16 [64, 1024], replicated, may hold values from -6 to 6
- out_weight: bfloat16 [1024, 1024], replicated, may hold values from -1.5 to 1.5
- out_bias: float32 [1024], replicated, may hold values from -3 to 3
- norm1_gain: float32 [1024], replicated, may hold values from 0.5 to 1.5
- norm1_shift: float32 [1024], replicated, may hold values from -3 to 3
- up_weight: bfloat16 [1024, 4096], P(None, 'mp'), may hold values from -0.1875 to 0.1875
- up_bias: bfloat16 [4096], P('mp'), may hold values from -3 to 3
- down_weight: bfloat16 [4096, 1024], P('mp'), may hold values from -0.09375 to 0.09375
- down_bias: float32 [1024], replicated, may hold values from -3 to 3
- norm2_gain: float32 [1024], replicated, may hold values from 0.5 to 1.5
- norm2_shift: float32 [1024], replicated, may hold values from -3 to 3
- out_grad: bfloat16 [32, 1024, 1024], P(('dp', 'mp')), may hold values from -6 to 6
Outputs:
- layer_out: bfloat16 [32, 1024, 1024], P(('dp', 'mp'))
- tokens_grad: bfloat16 [32, 1024, 1024], P(('dp', 'mp'))
- prefix_keys_grad: float32 [64, 1024], replicated
- prefix_values_grad: float32 [64, 1024], replicated
Inputs may be any that keep to these rules, and one draw needn't show every extreme that they name: `segment_ids`: in every row the ids run from 0 to 15 without falling, each sentence 1 to 128 tokens, one of them exactly 128.
All inputs are finite; a program needn't handle non-finite values.
Results may differ from a plain program's by a relative error of at most 0.012.
Values may be sent and summed in bfloat16 or wider, within the bound.
A program may use at most 256 MiB of HBM per device.

v0:
```python
import math

import jax
import jax.numpy as jnp
from jax import lax
from jax.sharding import PartitionSpec as P

HEADS = 16
HEAD_DIM = 64
PRE = 64


EPSILON = 1e-05
ROOT_HALF = 0.7071067811865476
INV_ROOT_TWOPI = 0.3989422804014327
MASK_FILL = -1e30


def gelu_act(values):
    return 0.5 * values * (1.0 + lax.erf(values * ROOT_HALF))


def gelu_slope(values):
    return (
        0.5 * (1.0 + lax.erf(values * ROOT_HALF))
        + values * jnp.exp(-0.5 * values * values) * INV_ROOT_TWOPI
    )


def norm_forward(values, norm_gain, norm_shift):
    average = jnp.mean(values, -1, keepdims=True)
    centred = values - average
    variance = jnp.mean(centred * centred, -1, keepdims=True)
    inverse_std = lax.rsqrt(variance + EPSILON)
    normed = centred * inverse_std
    return (normed * norm_gain + norm_shift, normed, inverse_std)


def norm_backward(grad_out, normed, inverse_std, norm_gain):
    scaled = grad_out * norm_gain
    first_mean = jnp.mean(scaled, -1, keepdims=True)
    second_mean = jnp.mean(scaled * normed, -1, keepdims=True)
    return (scaled - first_mean - normed * second_mean) * inverse_std


def split_row(joined_row, pre_keys, pre_vals):
    length = joined_row.shape[0]
    width = pre_keys.shape[1]
    queries = joined_row[:, :width].reshape(length, HEADS, HEAD_DIM)
    keys_all = jnp.concatenate([pre_keys, joined_row[:, width : 2 * width]], axis=0).reshape(
        PRE + length, HEADS, HEAD_DIM
    )
    vals_all = jnp.concatenate([pre_vals, joined_row[:, 2 * width :]], axis=0).reshape(
        PRE + length, HEADS, HEAD_DIM
    )
    return (queries, keys_all, vals_all)


def block_scores(query_block, seg_block, keys_all, seg_row):
    scale = 1.0 / math.sqrt(HEAD_DIM)
    scores = (
        jnp.einsum("qhd,khd->hqk", query_block, keys_all, preferred_element_type=jnp.float32)
        * scale
    )
    visible = jnp.concatenate(
        [jnp.ones((seg_block.shape[0], PRE), bool), seg_block[:, None] == seg_row[None, :]], axis=1
    )
    return jnp.where(visible[None], scores, MASK_FILL)


def attend_forward(joined_row, seg_row, pre_keys, pre_vals):
    queries, keys_all, vals_all = split_row(joined_row, pre_keys, pre_vals)
    length = joined_row.shape[0]
    width = pre_keys.shape[1]
    block = min(512, length)

    def one_block(index):
        start = index * block
        query_block = lax.dynamic_slice_in_dim(queries, start, block, 0)
        seg_block = lax.dynamic_slice_in_dim(seg_row, start, block, 0)
        scores = block_scores(query_block, seg_block, keys_all, seg_row)
        highest = jnp.max(scores, -1, keepdims=True)
        expo = jnp.exp(scores - highest)
        total = jnp.sum(expo, -1, keepdims=True)
        probs = (expo / total).astype(jnp.bfloat16)
        result = jnp.einsum("hqk,khd->qhd", probs, vals_all, preferred_element_type=jnp.float32)
        return (
            result.reshape(block, width).astype(jnp.bfloat16),
            (highest + jnp.log(total))[..., 0],
        )

    results, log_sums = lax.map(one_block, jnp.arange(length // block))
    return (results.reshape(length, width), log_sums)


def attend_backward(joined_row, seg_row, pre_keys, pre_vals, grad_row, log_sums):
    queries, keys_all, vals_all = split_row(joined_row, pre_keys, pre_vals)
    length = joined_row.shape[0]
    width = pre_keys.shape[1]
    block = min(512, length)
    scale = 1.0 / math.sqrt(HEAD_DIM)
    grad_heads = grad_row.reshape(length, HEADS, HEAD_DIM)

    def one_block(carry, index):
        grad_keys, grad_vals = carry
        start = index * block
        query_block = lax.dynamic_slice_in_dim(queries, start, block, 0)
        seg_block = lax.dynamic_slice_in_dim(seg_row, start, block, 0)
        grad_block = lax.dynamic_slice_in_dim(grad_heads, start, block, 0)
        scores = block_scores(query_block, seg_block, keys_all, seg_row)
        probs = jnp.exp(scores - log_sums[index][..., None])
        grad_probs = jnp.einsum(
            "qhd,khd->hqk", grad_block, vals_all, preferred_element_type=jnp.float32
        )
        delta = jnp.sum(probs * grad_probs, -1, keepdims=True)
        grad_scores = (probs * (grad_probs - delta)).astype(jnp.bfloat16)
        grad_query = (
            jnp.einsum("hqk,khd->qhd", grad_scores, keys_all, preferred_element_type=jnp.float32)
            * scale
        )
        grad_keys = (
            grad_keys
            + jnp.einsum(
                "hqk,qhd->khd", grad_scores, query_block, preferred_element_type=jnp.float32
            )
            * scale
        )
        grad_vals = grad_vals + jnp.einsum(
            "hqk,qhd->khd",
            probs.astype(jnp.bfloat16),
            grad_block,
            preferred_element_type=jnp.float32,
        )
        return ((grad_keys, grad_vals), grad_query)

    zeros_all = jnp.zeros((PRE + length, HEADS, HEAD_DIM), jnp.float32)
    (grad_keys, grad_vals), grad_queries = lax.scan(
        one_block, (zeros_all, zeros_all), jnp.arange(length // block)
    )
    grad_keys = grad_keys.reshape(PRE + length, width)
    grad_vals = grad_vals.reshape(PRE + length, width)
    grad_joined = jnp.concatenate(
        [grad_queries.reshape(length, width), grad_keys[PRE:], grad_vals[PRE:]], axis=1
    ).astype(jnp.bfloat16)
    return (grad_joined, grad_keys[:PRE], grad_vals[:PRE])


def on_device(
    tokens,
    segment_ids,
    qkv_weight,
    prefix_keys,
    prefix_values,
    out_weight,
    out_bias,
    norm1_gain,
    norm1_shift,
    up_weight,
    up_bias,
    down_weight,
    down_bias,
    norm2_gain,
    norm2_shift,
    out_grad,
):
    rows, length, width = tokens.shape
    count = rows * length
    flat_x = tokens.reshape(count, width)
    joined = jnp.dot(flat_x, qkv_weight, preferred_element_type=jnp.float32).astype(jnp.bfloat16)
    joined_rows = joined.reshape(rows, length, 3 * width)

    def row_attend(items):
        return attend_forward(items[0], items[1], prefix_keys, prefix_values)

    mixed, log_sums = lax.map(row_attend, (joined_rows, segment_ids))
    mixed = mixed.reshape(count, width)
    residual_one = (
        flat_x.astype(jnp.float32)
        + jnp.dot(mixed, out_weight, preferred_element_type=jnp.float32)
        + out_bias
    )
    first, first_hat, first_inv = norm_forward(residual_one, norm1_gain, norm1_shift)
    first_low = first.astype(jnp.bfloat16)
    up_all, bias_all, down_all = (
        lax.all_gather(up_weight, "mp", axis=1, tiled=True),
        lax.all_gather(up_bias, "mp", axis=0, tiled=True),
        lax.all_gather(down_weight, "mp", axis=0, tiled=True),
    )
    pre_act = jnp.dot(first_low, up_all, preferred_element_type=jnp.float32) + bias_all.astype(
        jnp.float32
    )
    hidden = gelu_act(pre_act).astype(jnp.bfloat16)
    branch = jnp.dot(hidden, down_all, preferred_element_type=jnp.float32) + down_bias
    residual_two = first + branch
    output, second_hat, second_inv = norm_forward(residual_two, norm2_gain, norm2_shift)
    grad_y = out_grad.reshape(count, width).astype(jnp.float32)
    grad_two = norm_backward(grad_y, second_hat, second_inv, norm2_gain)
    grad_branch = grad_two.astype(jnp.bfloat16)
    up_back, down_back = (
        lax.all_gather(up_weight, "mp", axis=1, tiled=True),
        lax.all_gather(down_weight, "mp", axis=0, tiled=True),
    )
    grad_hidden = lax.dot_general(
        grad_branch, down_back, (((1,), (1,)), ((), ())), preferred_element_type=jnp.float32
    )
    grad_pre = (grad_hidden * gelu_slope(pre_act)).astype(jnp.bfloat16)
    grad_ffn = lax.dot_general(
        grad_pre, up_back, (((1,), (1,)), ((), ())), preferred_element_type=jnp.float32
    )
    grad_first = grad_two + grad_ffn
    grad_one = norm_backward(grad_first, first_hat, first_inv, norm1_gain)
    grad_attn = grad_one.astype(jnp.bfloat16)
    grad_mixed = lax.dot_general(
        grad_attn, out_weight, (((1,), (1,)), ((), ())), preferred_element_type=jnp.float32
    ).astype(jnp.bfloat16)
    grad_mixed_rows = grad_mixed.reshape(rows, length, width)

    def row_back(carry, items):
        joined_row, seg_row, grad_row, sums_row = items
        grad_joined_row, grad_pk, grad_pv = attend_backward(
            joined_row, seg_row, prefix_keys, prefix_values, grad_row, sums_row
        )
        return ((carry[0] + grad_pk, carry[1] + grad_pv), grad_joined_row)

    zeros_pre = jnp.zeros((PRE, width), jnp.float32)
    (local_k, local_v), grad_joined = lax.scan(
        row_back, (zeros_pre, zeros_pre), (joined_rows, segment_ids, grad_mixed_rows, log_sums)
    )
    grad_joined = grad_joined.reshape(count, 3 * width)
    grad_tokens = grad_one + lax.dot_general(
        grad_joined, qkv_weight, (((1,), (1,)), ((), ())), preferred_element_type=jnp.float32
    )
    total_k, total_v = lax.psum((local_k, local_v), ("dp", "mp"))
    return (
        output.astype(jnp.bfloat16).reshape(rows, length, width),
        grad_tokens.astype(jnp.bfloat16).reshape(rows, length, width),
        total_k,
        total_v,
    )


def solution(mesh):
    return jax.shard_map(
        on_device,
        mesh=mesh,
        in_specs=(
            P(("dp", "mp"), None, None),
            P(("dp", "mp"), None),
            P(),
            P(),
            P(),
            P(),
            P(),
            P(),
            P(),
            P(None, "mp"),
            P("mp"),
            P("mp", None),
            P(),
            P(),
            P(),
            P(("dp", "mp"), None, None),
        ),
        out_specs=(P(("dp", "mp"), None, None), P(("dp", "mp"), None, None), P(), P()),
        check_vma=False,
    )
```

profile of v0, /device:TPU:0, one launch (start us, length us, event | category | flops | bytes accessed | tf_op | source)
XLA Modules:
  0.0 654.1 jit_solution(9765407117731093908)
XLA Ops:
  7.2 0.7 all-gather.4.cloned.1.call-update
  8.0 0.7 all-gather.6.cloned.1.call-update
  8.8 4.0 copy.45
  12.7 9.4 %convolution_convert_fusion = bf16[1024,3072]{1,0:T(8,128)(2,1)S(1)} fusion(bf16[1024,3072]{1,0:T(8,128)(2,1)} %param.22, bf16[1,1024,1024]{2,1,0:T(8,128)(2,1)} %param.20), kind=kOutput, calls=%fused_computation.58 | convolution fusion | flops 6445596672 | bytes 14680064 | tf_op jit(solution)/shard_map/dot_general | solution.py:169
  22.1 2.3 fusion.85
  24.4 2.6 pad_maximum_fusion
  27.0 4.2 copy.47
  31.1 4.2 copy.48
  35.4 4.0 copy.46
  39.3 23.8 %all-gather = bf16[16,1,256]{2,1,0:T(2,128)(2,1)S(1)} all-gather(bf16[1,1,256]{2,1,0:T(2,128)(2,1)S(1)} %reshape.180), channel_id=1, replica_groups=mesh['dp'=2,'mp'=16] {'mp'}, dimensions={0}, use_global_device_ids=true | all-gather | bytes 8704 | tf_op jit(solution)/shard_map/all_gather | solution.py:186
  63.1 0.6 convert_element_type.81
  63.8 3.9 copy.50
  67.7 108.5 %while.47 = (s32[]{:T(128)}, bf16[2,512,1024]{2,1,0:T(8,128)(2,1)}, f32[2,16,512]{2,1,0:T(8,128)S(1)}, s32[2]{0:T(128)S(1)}, s32[1024]{0:T(1024)S(1)}, /*index=5...) while((s32[]{:T(128)}, bf16[2,512,1024]{2,1,0:T(8,128)(2,1)}, ...), condition=%wide.region_3.4_spmd, body=%wide.region_0.3_spmd.sunk | while | flops 2389696512 | bytes 121383616 | solution.py:92
  67.7 0.6 dynamic_slice.72
  69.7 16.4 %fusion.131 = (f32[16,512]{1,0:T(8,128)S(1)}, f32[16,512,1088]{1,2,0:T(8,128)}) fusion(pred[512,1088]{0,1:T(8,128)(4,1)S(1)} %concatenate.30, bf16[1088,16,64]{0,2,1:T(8,128)(2,1)} %get-tuple-element.444, bf16[1024,16,64]{0,2,1:T(8,128)(2,1)} %get-tuple-element.443, s32[]{:T(128)S(6)} %select_n.44), kind=kOutput, calls=%fused_computation.3.clone.1 | convolution fusion | flops 1167581184 | bytes 39649284 | tf_op jit(solution)/shard_map/while/body/eval_jaxpr/while/body/eval_jaxpr/qhd,khd->hqk/dot_general | solution.py:62
  86.2 15.5 %fusion.132 = f32[16,512]{1,0:T(8,128)S(1)} fusion(f32[16,512,1088]{1,2,0:T(8,128)} %get-tuple-element.397, f32[16,512]{1,0:T(8,128)S(1)} %get-tuple-element.398, pred[512,1088]{0,1:T(8,128)(4,1)S(1)} %concatenate.30), kind=kLoop, calls=%fused_computation.4.clone.1 | loop fusion | flops 35643392 | bytes 36274176 | tf_op jit(solution)/shard_map/while/body/eval_jaxpr/while/body/eval_jaxpr/reduce_sum | solution.py:84
  101.7 17.5 %fusion.133 = bf16[16,512,64]{1,2,0:T(8,128)(2,1)} fusion(bf16[1088,16,64]{0,2,1:T(8,128)(2,1)} %get-tuple-element.445, f32[16,512,1088]{1,2,0:T(8,128)} %get-tuple-element.397, f32[16,512]{1,0:T(8,128)S(1)} %fusion.132, f32[16,512]{1,0:T(8,128)S(1)} %get-tuple-element.398, pred[512,1088]{0,1:T(8,128)(4,1)S(1)} %concatenate.30), kind=kOutput, calls=%fused_computation.6.clone.1 | convolution fusion | flops 1185939456 | bytes 39550976 | tf_op jit(solution)/shard_map/while/body/eval_jaxpr/while/body/eval_jaxpr/hqk,khd->qhd/dot_general | solution.py:86
  119.2 1.5 copy.64
  120.7 1.0 constant_dynamic-update-slice_fusion.2
  121.7 0.6 dynamic_slice.72
  123.7 16.9 %fusion.131 = (f32[16,512]{1,0:T(8,128)S(1)}, f32[16,512,1088]{1,2,0:T(8,128)}) fusion(pred[512,1088]{0,1:T(8,128)(4,1)S(1)} %concatenate.30, bf16[1088,16,64]{0,2,1:T(8,128)(2,1)} %get-tuple-element.444, bf16[1024,16,64]{0,2,1:T(8,128)(2,1)} %get-tuple-element.443, s32[]{:T(128)S(6)} %select_n.44), kind=kOutput, calls=%fused_computation.3.clone.1 | convolution fusion | flops 1167581184 | bytes 39649284 | tf_op jit(solution)/shard_map/while/body/eval_jaxpr/while/body/eval_jaxpr/qhd,khd->hqk/dot_general | solution.py:62
  140.6 15.0 %fusion.132 = f32[16,512]{1,0:T(8,128)S(1)} fusion(f32[16,512,1088]{1,2,0:T(8,128)} %get-tuple-element.397, f32[16,512]{1,0:T(8,128)S(1)} %get-tuple-element.398, pred[512,1088]{0,1:T(8,128)(4,1)S(1)} %concatenate.30), kind=kLoop, calls=%fused_computation.4.clone.1 | loop fusion | flops 35643392 | bytes 36274176 | tf_op jit(solution)/shard_map/while/body/eval_jaxpr/while/body/eval_jaxpr/reduce_sum | solution.py:84
  155.6 17.9 %fusion.133 = bf16[16,512,64]{1,2,0:T(8,128)(2,1)} fusion(bf16[1088,16,64]{0,2,1:T(8,128)(2,1)} %get-tuple-element.445, f32[16,512,1088]{1,2,0:T(8,128)} %get-tuple-element.397, f32[16,512]{1,0:T(8,128)S(1)} %fusion.132, f32[16,512]{1,0:T(8,128)S(1)} %get-tuple-element.398, pred[512,1088]{0,1:T(8,128)(4,1)S(1)} %concatenate.30), kind=kOutput, calls=%fused_computation.6.clone.1 | convolution fusion | flops 1185939456 | bytes 39550976 | tf_op jit(solution)/shard_map/while/body/eval_jaxpr/while/body/eval_jaxpr/hqk,khd->qhd/dot_general | solution.py:86
  173.5 1.5 copy.64
  175.0 1.0 constant_dynamic-update-slice_fusion.2
  176.2 5.0 fusion.86
  181.3 1.9 copy-done.8
  183.8 16.8 %fusion.49 = f32[1024,4096]{1,0:T(8,128)} fusion(bf16[1024,4096]{1,0:T(8,128)(2,1)} %all-gather.4.cloned.1.call-done, f32[1024,1024]{0,1:T(8,128)} %copy-done.8, f32[1024]{0:T(1024)S(1)} %copy-done.28, f32[1024]{0:T(1024)S(1)} %copy-done.29, f32[1024]{0:T(1024)S(1)} %add_rsqrt_fusion.1, f32[1024]{0:T(1024)S(1)} %broadcast_multiply_fusion.5), kind=kOutput, calls=%fused_computation.83 | convolution fusion | flops 8595177472 | bytes 29376512 | tf_op jit(solution)/shard_map/dot_general | solution.py:189
  200.6 17.8 %fusion.87 = (f32[1024]{0:T(1024)S(1)}, f32[1024,1024]{0,1:T(8,128)}) fusion(f32[1024]{0:T(1024)S(1)} %copy-done.27, bf16[4096,1024]{1,0:T(8,128)(2,1)} %all-gather.6.cloned.1.call-done, f32[1024,4096]{1,0:T(8,128)} %fusion.49, f32[4096]{0:T(1024)S(1)} %bitcast.122, f32[1024]{0:T(1024)S(1)} %copy-done.28, f32[1024]{0:T(1024)S(1)} %copy-done.29, ...), kind=kOutput, calls=%fused_computation.116 | convolution fusion | flops 8622439424 | bytes 33595392 | tf_op jit(solution)/shard_map/dot_general | solution.py:193
  218.4 2.8 multiply_reduce_fusion.2
  221.3 0.6 copy-done.6
  221.9 4.1 fusion.44
  225.9 21.4 %fusion.27.clone.3.clone.4 = bf16[1024,4096]{1,0:T(8,128)(2,1)} fusion(f32[1024,4096]{1,0:T(8,128)} %fusion.49, bf16[4096,1024]{1,0:T(8,128)(2,1)} %all-gather.6.cloned.1.call-done, f32[4096]{0:T(1024)S(1)} %bitcast.123, f32[1024,1024]{0,1:T(8,128)S(1)} %copy-done.6, bf16[1,1024,1024]{1,2,0:T(8,128)(2,1)S(1)} %copy-done.7, ...), kind=kOutput, calls=%fused_computation.41.clone.clone.clone.clone.clone.clone.clone.1 | convolution fusion | flops 8645509120 | bytes 39882752 | tf_op jit(solution)/shard_map/dot_general | solution.py:203
  247.3 16.6 %fusion.84 = (f32[1024]{0:T(1024)S(1)}, f32[1024]{0:T(1024)S(1)}, f32[1024,1024]{0,1:T(8,128)S(1)}) fusion(f32[1024]{0:T(1024)S(1)} %add_rsqrt_fusion.1, f32[1024,1024]{0,1:T(8,128)} %copy-done.8, f32[1024]{0:T(1024)S(1)} %broadcast_multiply_fusion.5, f32[1024]{0:T(1024)S(1)} %copy-done.29, bf16[1024,4096]{1,0:T(8,128)(2,1)} %all-gather.4.cloned.1.call-done, ...), kind=kOutput, calls=%fused_computation.113 | convolution fusion | flops 8605661184 | bytes 31498240 | tf_op jit(solution)/shard_map/dot_general | solution.py:207
  264.0 3.8 fusion.76
  267.9 234.6 %while.48 = (s32[]{:T(128)}, f32[1088,16,64]{0,2,1:T(8,128)}, f32[1088,16,64]{0,2,1:T(8,128)}, bf16[2,512,16,64]{1,3,2,0:T(8,128)(2,1)}, s32[2]{0:T(128)S(1)}, /...) while((s32[]{:T(128)}, f32[1088,16,64]{0,2,1:T(8,128)}, ...), condition=%wide.region_14.15_spmd.clone, body=%wide.region_12.14_spmd.clone.sunk | while | flops 5791080448 | bytes 343255456 | solution.py:137
  268.1 0.6 dynamic_slice.79
  269.3 18.7 %fusion.143 = f32[16,512,1088]{1,2,0:T(8,128)} fusion(bf16[1088,16,64]{0,2,1:T(8,128)(2,1)} %get-tuple-element.495, bf16[1024,16,64]{0,2,1:T(8,128)(2,1)} %get-tuple-element.494, s32[]{:T(128)S(6)} %select_n.45), kind=kOutput, calls=%fused_computation.26.clone.1 | convolution fusion | flops 1140850688 | bytes 39059460 | tf_op jit(solution)/shard_map/while/body/eval_jaxpr/while/body/eval_jaxpr/qhd,khd->hqk/dot_general | solution.py:112
  290.6 27.0 %multiply_reduce_fusion.5 = (f32[16,512]{1,0:T(8,128)S(1)}, f32[16,512,1088]{1,2,0:T(8,128)}) fusion(f32[16,512,1088]{1,2,0:T(8,128)} %fusion.143, f32[16,512]{1,0:T(8,128)S(1)} %dynamic-slice_bitcast_fusion.2, bf16[1088,16,64]{0,2,1:T(8,128)(2,1)} %get-tuple-element.492, bf16[1024,16,64]{0,2,1:T(8,128)(2,1)S(1)} %copy-done.4, s32[]{:T(128)S(6)} %select_n.45, ...), kind=kOutput, calls=%fused_computation.16.clone.1 | convolution fusion | flops 1185406976 | bytes 75202560 | tf_op jit(solution)/shard_map/while/body/eval_jaxpr/while/body/eval_jaxpr/qhd,khd->hqk/dot_general | solution.py:62
  317.7 29.4 %multiply_convert_fusion.6 = bf16[16,512,1088]{1,2,0:T(8,128)(2,1)} fusion(f32[16,512,1088]{1,2,0:T(8,128)} %get-tuple-element.410, f32[16,512,1088]{1,2,0:T(8,128)} %fusion.143, f32[16,512]{1,0:T(8,128)S(1)} %get-tuple-element.411), kind=kLoop, calls=%fused_computation.15.clone.1 | loop fusion | flops 26738688 | bytes 89161728 | tf_op jit(solution)/shard_map/while/body/eval_jaxpr/while/body/eval_jaxpr/convert_element_type | solution.py:116
  347.1 10.6 %bitcast_add_fusion.4 = f32[1088,16,64]{0,2,1:T(8,128)} fusion(f32[1088,16,64]{0,2,1:T(8,128)} %get-tuple-element.469, bf16[16,512,1088]{1,2,0:T(8,128)(2,1)} %multiply_convert_fusion.6, pred[]{:T(512)S(6)} %compare.5, bf16[1024,16,64]{0,2,1:T(8,128)(2,1)S(1)} %copy-done.4, s32[]{:T(128)S(6)} %select_n.45), kind=kOutput, calls=%fused_computation.22.clone.1 | convolution fusion | flops 1144193024 | bytes 27787268 | tf_op jit(solution)/shard_map/while/body/eval_jaxpr/while/body/eval_jaxpr/hqk,qhd->khd/dot_general | solution.py:123
  357.7 9.5 %bitcast_dynamic-update-slice_fusion.5 = bf16[2,512,16,64]{1,3,2,0:T(8,128)(2,1)S(1)} fusion(bf16[2,512,16,64]{1,3,2,0:T(8,128)(2,1)S(1)} %copy-done.10, s32[]{:T(128)} %get-tuple-element.468, bf16[1088,16,64]{0,2,1:T(8,128)(2,1)S(1)} %copy-done.2, bf16[16,512,1088]{1,2,0:T(8,128)(2,1)} %multiply_convert_fusion.6), kind=kOutput, calls=%fused_computation.23.clone.1 | convolution fusion | flops 1141374976 | bytes 22282244 | tf_op jit(solution)/shard_map/while/body/eval_jaxpr/while/body/eval_jaxpr/hqk,khd->qhd/dot_general | solution.py:118
  367.2 1.3 copy-done.11
  368.5 15.5 %bitcast_add_fusion.5 = f32[1088,16,64]{0,2,1:T(8,128)} fusion(f32[1088,16,64]{0,2,1:T(8,128)} %get-tuple-element.470, f32[16,512,1088]{1,2,0:T(8,128)} %get-tuple-element.410, pred[]{:T(512)S(6)} %compare.5, bf16[1024,16,64]{0,2,1:T(8,128)(2,1)S(1)} %copy-done.5, s32[]{:T(128)S(6)} %select_n.45), kind=kOutput, calls=%fused_computation.21.clone.1 | convolution fusion | flops 1151991808 | bytes 45613060 | tf_op jit(solution)/shard_map/while/body/eval_jaxpr/while/body/eval_jaxpr/hqk,qhd->khd/dot_general | solution.py:128
  385.2 18.7 %fusion.143 = f32[16,512,1088]{1,2,0:T(8,128)} fusion(bf16[1088,16,64]{0,2,1:T(8,128)(2,1)} %get-tuple-element.495, bf16[1024,16,64]{0,2,1:T(8,128)(2,1)} %get-tuple-element.494, s32[]{:T(128)S(6)} %select_n.45), kind=kOutput, calls=%fused_computation.26.clone.1 | convolution fusion | flops 1140850688 | bytes 39059460 | tf_op jit(solution)/shard_map/while/body/eval_jaxpr/while/body/eval_jaxpr/qhd,khd->hqk/dot_general | solution.py:112
  406.5 27.1 %multiply_reduce_fusion.5 = (f32[16,512]{1,0:T(8,128)S(1)}, f32[16,512,1088]{1,2,0:T(8,128)}) fusion(f32[16,512,1088]{1,2,0:T(8,128)} %fusion.143, f32[16,512]{1,0:T(8,128)S(1)} %dynamic-slice_bitcast_fusion.2, bf16[1088,16,64]{0,2,1:T(8,128)(2,1)} %get-tuple-element.492, bf16[1024,16,64]{0,2,1:T(8,128)(2,1)S(1)} %copy-done.4, s32[]{:T(128)S(6)} %select_n.45, ...), kind=kOutput, calls=%fused_computation.16.clone.1 | convolution fusion | flops 1185406976 | bytes 75202560 | tf_op jit(solution)/shard_map/while/body/eval_jaxpr/while/body/eval_jaxpr/qhd,khd->hqk/dot_general | solution.py:62
  433.6 29.4 %multiply_convert_fusion.6 = bf16[16,512,1088]{1,2,0:T(8,128)(2,1)} fusion(f32[16,512,1088]{1,2,0:T(8,128)} %get-tuple-element.410, f32[16,512,1088]{1,2,0:T(8,128)} %fusion.143, f32[16,512]{1,0:T(8,128)S(1)} %get-tuple-element.411), kind=kLoop, calls=%fused_computation.15.clone.1 | loop fusion | flops 26738688 | bytes 89161728 | tf_op jit(solution)/shard_map/while/body/eval_jaxpr/while/body/eval_jaxpr/convert_element_type | solution.py:116
  463.0 11.7 %bitcast_add_fusion.4 = f32[1088,16,64]{0,2,1:T(8,128)} fusion(f32[1088,16,64]{0,2,1:T(8,128)} %get-tuple-element.469, bf16[16,512,1088]{1,2,0:T(8,128)(2,1)} %multiply_convert_fusion.6, pred[]{:T(512)S(6)} %compare.5, bf16[1024,16,64]{0,2,1:T(8,128)(2,1)S(1)} %copy-done.4, s32[]{:T(128)S(6)} %select_n.45), kind=kOutput, calls=%fused_computation.22.clone.1 | convolution fusion | flops 1144193024 | bytes 27787268 | tf_op jit(solution)/shard_map/while/body/eval_jaxpr/while/body/eval_jaxpr/hqk,qhd->khd/dot_general | solution.py:123
  474.7 9.5 %bitcast_dynamic-update-slice_fusion.5 = bf16[2,512,16,64]{1,3,2,0:T(8,128)(2,1)S(1)} fusion(bf16[2,512,16,64]{1,3,2,0:T(8,128)(2,1)S(1)} %copy-done.10, s32[]{:T(128)} %get-tuple-element.468, bf16[1088,16,64]{0,2,1:T(8,128)(2,1)S(1)} %copy-done.2, bf16[16,512,1088]{1,2,0:T(8,128)(2,1)} %multiply_convert_fusion.6), kind=kOutput, calls=%fused_computation.23.clone.1 | convolution fusion | flops 1141374976 | bytes 22282244 | tf_op jit(solution)/shard_map/while/body/eval_jaxpr/while/body/eval_jaxpr/hqk,khd->qhd/dot_general | solution.py:118
  484.2 1.3 copy-done.11
  485.6 16.7 %bitcast_add_fusion.5 = f32[1088,16,64]{0,2,1:T(8,128)} fusion(f32[1088,16,64]{0,2,1:T(8,128)} %get-tuple-element.470, f32[16,512,1088]{1,2,0:T(8,128)} %get-tuple-element.410, pred[]{:T(512)S(6)} %compare.5, bf16[1024,16,64]{0,2,1:T(8,128)(2,1)S(1)} %copy-done.5, s32[]{:T(128)S(6)} %select_n.45), kind=kOutput, calls=%fused_computation.21.clone.1 | convolution fusion | flops 1151991808 | bytes 45613060 | tf_op jit(solution)/shard_map/while/body/eval_jaxpr/while/body/eval_jaxpr/hqk,qhd->khd/dot_general | solution.py:128
  502.5 1.2 slice.55
  503.7 4.7 slice.67
  508.4 2.0 slice.66
  510.5 0.9 copy.58
  511.4 0.9 copy.59
  512.3 3.8 copy.51
  516.0 2.0 copy.62
  518.1 13.6 %fusion.52 = bf16[1,1024,1024]{1,2,0:T(8,128)(2,1)} fusion(bf16[1024,3072]{1,0:T(8,128)(2,1)} %param.22, bf16[1024,1024]{0,1:T(8,128)(2,1)} %bitcast.117, bf16[1024,1024]{0,1:T(8,128)(2,1)} %bitcast.116, bf16[1024,1024]{0,1:T(8,128)(2,1)} %bitcast.118, f32[1024]{0:T(1024)S(1)} %copy-done.23, f32[1024]{0:T(1024)S(1)} %copy-done.21, ...), kind=kOutput, calls=%fused_computation.85 | convolution fusion | flops 6469713920 | bytes 23085056 | tf_op jit(solution)/shard_map/dot_general | solution.py:230
  531.7 3.9 copy.56
  535.6 3.9 copy.55
  539.6 104.4 %all-reduce.5.cloned.1.call-done = (f32[64,1024]{1,0:T(8,128)}, f32[64,1024]{1,0:T(8,128)}) async-done(((f32[64,1024]{1,0:T(8,128)}, f32[64,1024]{1,0:T(8,128)}), (f32[64,1024]{1,0:T(8,128)}, f32[64,1024]{1,0:T(8,128)})) %all-reduce.5.cloned.1.call-update) | async-done | bytes 524304 | tf_op jit(solution)/shard_map/psum | solution.py:233
  644.0 1.7 copy.91
  645.7 1.7 copy.92
  (111 shorter events, 4.0 us)
Async XLA Ops:
  7.2 169.0 %copy-start = (bf16[1024,1024]{1,0:T(8,128)(2,1)S(1)}, bf16[1024,1024]{1,0:T(8,128)(2,1)}, u32[]{:S(2)}) copy-start(bf16[1024,1024]{1,0:T(8,128)(2,1)} %param.25) | copy-start | bytes 6291460
  7.2 176.6 %all-gather.4.cloned.1.call-start = ((), (), s32[]{:S(2)}) async-start(), calls=%async_computation | async-start | bytes 8912896 | tf_op jit(solution)/shard_map/all_gather | solution.py:185
  7.9 192.7 %all-gather.6.cloned.1.call-start = ((), (), s32[]{:S(2)}) async-start(), calls=%async_computation.1 | async-start | bytes 8912896 | tf_op jit(solution)/shard_map/all_gather | solution.py:187
  8.7 635.3 %all-reduce.5.cloned.1.call-start = ((), (), s32[]{:S(2)}) async-start(), calls=%async_computation.2 | async-start | bytes 1048576 | tf_op jit(solution)/shard_map/psum | solution.py:233
  22.1 2.3 copy-start.13
  22.1 2.3 copy-start.14
  31.1 8.2 %copy-start.30 = (bf16[256]{0:T(256)(128)(2,1)S(1)}, bf16[256]{0:T(256)(128)(2,1)}, u32[]{:S(2)}) copy-start(bf16[256]{0:T(256)(128)(2,1)} %param.30) | copy-start | bytes 1540
  35.4 32.4 %copy-start.12 = (s32[1,1024]{1,0:T(1,128)S(1)}, s32[1,1024]{1,0:T(1,128)}, u32[]{:S(2)}) copy-start(s32[1,1024]{1,0:T(1,128)} %param.21) | copy-start | bytes 12292
  67.7 108.5 %copy-start.26 = (f32[1024]{0:T(1024)S(1)}, f32[1024]{0:T(1024)}, u32[]{:S(2)}) copy-start(f32[1024]{0:T(1024)} %param.26) | copy-start | bytes 12292
  181.3 2.0 copy-start.8
  181.3 2.5 copy-start.28
  181.3 2.5 copy-start.29
  181.3 82.7 %copy-start.16 = (f32[1024]{0:T(1024)}, f32[1024]{0:T(1024)S(1)}, u32[]{:S(2)}) copy-start(f32[1024]{0:T(1024)S(1)} %broadcast_multiply_fusion.5) | copy-start | bytes 12292
  183.7 80.3 %copy-start.20 = (f32[1024]{0:T(1024)}, f32[1024]{0:T(1024)S(1)}, u32[]{:S(2)}) copy-start(f32[1024]{0:T(1024)S(1)} %add_rsqrt_fusion.1) | copy-start | bytes 12292
  183.7 16.9 %copy-start.15 = (f32[16,1,256]{2,1,0:T(1,128)S(1)}, f32[16,1,256]{2,1,0:T(1,128)}, u32[]{:S(2)}) copy-start(f32[16,1,256]{2,1,0:T(1,128)} %convert_element_type.81) | copy-start | bytes 49156
  183.8 16.9 %copy-start.27 = (f32[1024]{0:T(1024)S(1)}, f32[1024]{0:T(1024)}, u32[]{:S(2)}) copy-start(f32[1024]{0:T(1024)} %param.32) | copy-start | bytes 12292
  218.4 3.4 copy-start.6
  218.4 3.4 copy-start.18
  218.4 3.5 copy-start.19
  221.9 4.1 copy-start.7
  247.3 16.7 %copy-start.9 = (f32[1024,1024]{0,1:T(8,128)S(1)}, f32[1024,1024]{0,1:T(8,128)}, u32[]{:S(2)}) copy-start(f32[1024,1024]{0,1:T(8,128)} %copy-done.8) | copy-start | bytes 12582916
  264.0 3.9 copy-start.31
  264.0 3.9 copy-start.22
  264.0 3.9 copy-start.24
  269.3 21.3 %copy-start.4 = (bf16[1024,16,64]{0,2,1:T(8,128)(2,1)S(1)}, bf16[1024,16,64]{0,2,1:T(8,128)(2,1)}, u32[]{:S(2)}) copy-start(bf16[1024,16,64]{0,2,1:T(8,128)(2,1)} %get-tuple-element.490) | copy-start | bytes 6291460 | tf_op jit(solution)/shard_map/while/body/eval_jaxpr/while
  347.1 10.6 %copy-start.2 = (bf16[1088,16,64]{0,2,1:T(8,128)(2,1)S(1)}, bf16[1088,16,64]{0,2,1:T(8,128)(2,1)}, u32[]{:S(2)}) copy-start(bf16[1088,16,64]{0,2,1:T(8,128)(2,1)} %get-tuple-element.492) | copy-start | bytes 6684676 | tf_op jit(solution)/shard_map/while/body/eval_jaxpr/while
  347.1 10.6 %copy-start.10 = (bf16[2,512,16,64]{1,3,2,0:T(8,128)(2,1)S(1)}, bf16[2,512,16,64]{1,3,2,0:T(8,128)(2,1)}, u32[]{:S(2)}) copy-start(bf16[2,512,16,64]{1,3,2,0:T(8,128)(2,1)} %get-tuple-element.471) | copy-start | bytes 6291460 | tf_op jit(solution)/shard_map/while/body/eval_jaxpr/while
  357.7 10.8 %copy-start.5 = (bf16[1024,16,64]{0,2,1:T(8,128)(2,1)S(1)}, bf16[1024,16,64]{0,2,1:T(8,128)(2,1)}, u32[]{:S(2)}) copy-start(bf16[1024,16,64]{0,2,1:T(8,128)(2,1)} %get-tuple-element.494) | copy-start | bytes 6291460 | tf_op jit(solution)/shard_map/while/body/eval_jaxpr/while
  367.2 1.3 copy-start.11
  385.2 21.3 %copy-start.4 = (bf16[1024,16,64]{0,2,1:T(8,128)(2,1)S(1)}, bf16[1024,16,64]{0,2,1:T(8,128)(2,1)}, u32[]{:S(2)}) copy-start(bf16[1024,16,64]{0,2,1:T(8,128)(2,1)} %get-tuple-element.490) | copy-start | bytes 6291460 | tf_op jit(solution)/shard_map/while/body/eval_jaxpr/while
  463.0 11.7 %copy-start.2 = (bf16[1088,16,64]{0,2,1:T(8,128)(2,1)S(1)}, bf16[1088,16,64]{0,2,1:T(8,128)(2,1)}, u32[]{:S(2)}) copy-start(bf16[1088,16,64]{0,2,1:T(8,128)(2,1)} %get-tuple-element.492) | copy-start | bytes 6684676 | tf_op jit(solution)/shard_map/while/body/eval_jaxpr/while
  463.0 11.7 %copy-start.10 = (bf16[2,512,16,64]{1,3,2,0:T(8,128)(2,1)S(1)}, bf16[2,512,16,64]{1,3,2,0:T(8,128)(2,1)}, u32[]{:S(2)}) copy-start(bf16[2,512,16,64]{1,3,2,0:T(8,128)(2,1)} %get-tuple-element.471) | copy-start | bytes 6291460 | tf_op jit(solution)/shard_map/while/body/eval_jaxpr/while
  474.7 10.8 %copy-start.5 = (bf16[1024,16,64]{0,2,1:T(8,128)(2,1)S(1)}, bf16[1024,16,64]{0,2,1:T(8,128)(2,1)}, u32[]{:S(2)}) copy-start(bf16[1024,16,64]{0,2,1:T(8,128)(2,1)} %get-tuple-element.494) | copy-start | bytes 6291460 | tf_op jit(solution)/shard_map/while/body/eval_jaxpr/while
  484.2 1.3 copy-start.11
  502.5 5.9 copy-start.3
  512.3 5.8 copy-start.17
  512.3 5.8 copy-start.21
  512.3 5.8 copy-start.23
  512.3 5.8 copy-start.25
  518.1 129.3 %copy-start.1 = (bf16[1024,1024]{1,0:T(8,128)(2,1)S(1)}, bf16[1024,1024]{1,0:T(8,128)(2,1)}, u32[]{:S(2)}) copy-start(bf16[1024,1024]{1,0:T(8,128)(2,1)} %param.25) | copy-start | bytes 6291460
Sparse Core Ops, SparseCore 0:
  10.2 80.8 all-gather.3
  93.2 73.0 all-gather.5
  518.1 125.7 all-reduce.4
where the time goes:
time: 659 us; the launch traced here: 654 us
  matrix products  338 us (51%)
  waiting for transfers between devices  106 us (16%)
  other arithmetic  101 us (15%)
  local copies, waits for them, and re-layouts  63.2 us (10%)
  blocking collectives  23.8 us (4%)
  between operations  14.4 us (2%)
  loops' own time  7.31 us (1%)
    psum x1, waiting for transfers between devices, on_device(): total_k, total_v = lax.psum((local_k, local_v), ('dp', 'mp'))  104 us
    dot_general x4, matrix products, block_scores(): jnp.einsum('qhd,khd->hqk', query_block, keys_all, preferred_element_type=...  87.4 us
    convert_element_type x2, other arithmetic, one_block(): grad_scores = (probs * (grad_probs - delta)).astype(jnp.bfloat16)  58.8 us
    dot_general x2, matrix products, one_block(): jnp.einsum('qhd,khd->hqk', grad_block, vals_all, preferred_element_type=j...  37.4 us
    dot_general x2, matrix products, one_block(): jnp.einsum('hqk,khd->qhd', probs, vals_all, preferred_element_type=jnp.fl...  35.4 us
    dot_general x2, matrix products, one_block(): jnp.einsum('hqk,qhd->khd', probs.astype(jnp.bfloat16), grad_block, prefer...  32.2 us
    reduce_sum x2, other arithmetic, one_block(): total = jnp.sum(expo, -1, keepdims=True)  30.5 us
    all_gather x1, blocking collectives, on_device(): lax.all_gather(up_bias, 'mp', axis=0, tiled=True)  23.8 us
  transfers between devices with their start and end apart: 3, of which 1 were waited for; matrix products, arithmetic and copies ran while one was open for 28% of the time, Pallas kernels for 0%

commit v1 on v0

v1 whole, which is shorter than its diff:
```python
import functools

import jax
import jax.numpy as jnp
from jax import lax
from jax.experimental import pallas as pl
from jax.experimental.pallas import tpu as pltpu
from jax.sharding import PartitionSpec as P

EPSILON = 1e-05
ROOT_HALF = 0.7071067811865476
INV_ROOT_TWOPI = 0.3989422804014327
MASK_FILL = -1e30
HEAD_DIM = 64
PAIR = 2 * HEAD_DIM
QB = 128
F32 = jnp.float32
BF16 = jnp.bfloat16
VMEM_LIMIT = 62 * 1024 * 1024


def dot(a, b):
    return lax.dot_general(a, b, (((1,), (0,)), ((), ())), preferred_element_type=F32)


def dot_t(a, b):
    return lax.dot_general(a, b, (((1,), (1,)), ((), ())), preferred_element_type=F32)


def eye(n):
    r = lax.broadcasted_iota(jnp.int32, (n, n), 0)
    c = lax.broadcasted_iota(jnp.int32, (n, n), 1)
    return jnp.where(r == c, 1.0, 0.0).astype(BF16)


def split_heads(x):
    lane = lax.broadcasted_iota(jnp.int32, x.shape, 1)
    zero = jnp.zeros_like(x)
    return jnp.concatenate([jnp.where(lane < HEAD_DIM, x, zero), jnp.where(lane < HEAD_DIM, zero, x)], axis=0)


def own_blocks(x):
    return jnp.concatenate([x[:HEAD_DIM, :QB], x[HEAD_DIM:, QB:]], axis=0)


def normalize(x):
    scale = 1.0 / x.shape[-1]
    cen = x - jnp.sum(x, -1, keepdims=True) * scale
    inv = lax.rsqrt(jnp.sum(cen * cen, -1, keepdims=True) * scale + EPSILON)
    return cen * inv, inv


def norm_back(grad, hat, inv, gain):
    scale = 1.0 / grad.shape[-1]
    sc = grad * gain
    mean1 = jnp.sum(sc, -1, keepdims=True) * scale
    mean2 = jnp.sum(sc * hat, -1, keepdims=True) * scale
    return (sc - mean1 - hat * mean2) * inv


def whole(a):
    return pl.BlockSpec(a.shape, lambda i: (0,) * a.ndim, pipeline_mode=pl.Buffered(1))


def kept(shape, dtype):
    spec = pl.BlockSpec(shape, lambda i: (0,) * len(shape), pipeline_mode=pl.Buffered(1))
    return spec, jax.ShapeDtypeStruct(shape, dtype)


def forward_kernel(tok_ref, wqkv_ref, seg_ref, pk_ref, pv_ref, wo_ref, bo_ref,
                   q_out, k_out, v_out, mix_out, p_out, res_out,
                   vt, pvt, segc, bias, sbuf, mixt):
    qb = pl.program_id(0)
    length, width = tok_ref.shape
    window = bias.shape[0]
    pairs = width // PAIR

    @pl.when(qb == 0)
    def _():
        tile = 256
        for part, ref in enumerate((q_out, k_out, v_out)):
            for j in range(width // tile):
                x = dot(tok_ref[...], wqkv_ref[:, part * width + j * tile:part * width + (j + 1) * tile]).astype(BF16)
                if part == 0:
                    x = x * jnp.asarray(HEAD_DIM ** -0.5, BF16)
                ref[:, j * tile:(j + 1) * tile] = x
        big = eye(256)
        for j in range(width // 256):
            cols = slice(j * 256, (j + 1) * 256)
            vt[cols, :] = dot_t(big, v_out[:, cols]).astype(BF16)
            pvt[cols, :] = dot_t(big, pv_ref[:, cols]).astype(BF16)
        ident = eye(QB)
        seg = jnp.broadcast_to(seg_ref[...].astype(F32), (QB, length)).astype(BF16)
        for j in range(length // QB):
            segc[j * QB:(j + 1) * QB, :] = dot_t(ident, seg[:, j * QB:(j + 1) * QB])

    start = pl.multiple_of(jnp.clip(qb * QB - QB, 0, length - window), QB)
    win = pl.ds(start, window)
    rows = pl.ds(pl.multiple_of(qb * QB, QB), QB)
    segq = seg_ref[:, rows].astype(F32)
    bias[...] = jnp.where(segc[win, :] == segq, 0.0, MASK_FILL)

    def score(pair):
        cols = slice(pair * PAIR, (pair + 1) * PAIR)
        keys = jnp.concatenate([k_out[win, cols], pk_ref[:, cols]], axis=0)
        sbuf[pair % 2] = dot_t(keys, split_heads(q_out[rows, cols]))

    def soft(pair):
        both = jnp.concatenate([bias[...], bias[...]], axis=1)
        sw = sbuf[pair % 2, :window] + both
        sp = sbuf[pair % 2, window:]
        top = jnp.maximum(jnp.max(sw, 0, keepdims=True), jnp.max(sp, 0, keepdims=True))
        ew = jnp.exp(sw - top)
        ep = jnp.exp(sp - top)
        inv = 1.0 / (jnp.sum(ew, 0, keepdims=True) + jnp.sum(ep, 0, keepdims=True))
        p_out[0, pair, :window] = (ew * inv).astype(BF16)
        p_out[0, pair, window:] = (ep * inv).astype(BF16)

    def mixing(pair):
        cols = slice(pair * PAIR, (pair + 1) * PAIR)
        vals = jnp.concatenate([vt[cols, win], pvt[cols, :]], axis=1)
        mixt[cols, rows] = own_blocks(dot(vals, p_out[0, pair])).astype(BF16)

    for i in range(pairs + 2):
        if i < pairs:
            score(i)
        if 0 <= i - 1 < pairs:
            soft(i - 1)
        if 0 <= i - 2 < pairs:
            mixing(i - 2)

    @pl.when(qb == pl.num_programs(0) - 1)
    def _():
        big = eye(256)
        for r in range(length // 256):
            rr = slice(r * 256, (r + 1) * 256)
            mix_out[rr] = dot_t(big, mixt[:, rr]).astype(BF16)
        for r in range(length // 256):
            rr = slice(r * 256, (r + 1) * 256)
            res_out[rr] = tok_ref[rr].astype(F32) + dot(mix_out[rr], wo_ref[...]) + bo_ref[...]


def attend_forward(tok, wqkv, seg, pk, pv, wo, bo):
    length, width = tok.shape
    pre = pk.shape[0]
    window = 3 * QB
    pairs, blocks = width // PAIR, length // QB
    outs = [kept((length, width), BF16)] * 4 + [
        (pl.BlockSpec((1, pairs, window + pre, 2 * QB), lambda i: (i, 0, 0, 0)),
         jax.ShapeDtypeStruct((blocks, pairs, window + pre, 2 * QB), BF16)),
        kept((length, width), F32)]
    return pl.pallas_call(
        forward_kernel,
        grid=(blocks,),
        in_specs=[whole(a) for a in (tok, wqkv, seg, pk, pv, wo, bo)],
        out_specs=[o[0] for o in outs],
        out_shape=[o[1] for o in outs],
        scratch_shapes=[
            pltpu.VMEM((width, length), BF16),
            pltpu.VMEM((width, pre), BF16),
            pltpu.VMEM((length, QB), F32),
            pltpu.VMEM((window, QB), F32),
            pltpu.VMEM((2, window + pre, 2 * QB), F32),
            pltpu.VMEM((width, length), BF16),
        ],
        compiler_params=pltpu.CompilerParams(vmem_limit_bytes=VMEM_LIMIT),
        name="attend_forward",
    )(tok, wqkv, seg, pk, pv, wo, bo)


def ffn_kernel(chunk, res_ref, dy_ref, up_hbm, down_hbm, ub_ref, wo_ref, db_ref, g1_ref, s1_ref, g2_ref, s2_ref,
               out_ref, gone_ref, gmix_ref, up, down, pre, hid, slope, low, acc, hat_s, sems):
    step = pl.program_id(0)
    count = up.shape[1] // chunk

    def fetch(j):
        cols = pl.ds(j * chunk, chunk)
        return (
            pltpu.make_async_copy(up_hbm.at[:, cols], up.at[:, cols], sems.at[0, j]),
            pltpu.make_async_copy(down_hbm.at[cols], down.at[cols], sems.at[1, j]),
        )

    @pl.when(step == 0)
    def _():
        for j in range(count):
            for copy in fetch(j):
                copy.start()
        for j in range(count):
            for copy in fetch(j):
                copy.wait()

    hat, inv1 = normalize(res_ref[...])
    hat_s[...] = hat
    low[...] = (hat * g1_ref[...] + s1_ref[...]).astype(BF16)

    def cols_of(j):
        return slice(j * chunk, (j + 1) * chunk)

    def rows_up(j):
        pre[j % 2] = dot(low[...], up[:, cols_of(j)])

    def act(j):
        u = pre[j % 2] + ub_ref[:, cols_of(j)].astype(F32)
        half = 0.5 * lax.erf(u * ROOT_HALF) + 0.5
        hid[j % 2] = (u * half).astype(BF16)
        slope[:, cols_of(j)] = (half + u * (jnp.exp(-0.5 * u * u) * INV_ROOT_TWOPI)).astype(BF16)

    def rows_down(j):
        acc[...] += dot(hid[j % 2], down[cols_of(j)])

    acc[...] = jnp.zeros_like(acc)
    for j in range(count + 2):
        if j < count:
            rows_up(j)
        if 0 <= j - 2 < count:
            rows_down(j - 2)
        if 0 <= j - 1 < count:
            act(j - 1)

    hat2, inv2 = normalize(hat_s[...] * g1_ref[...] + s1_ref[...] + acc[...] + db_ref[...])
    out_ref[...] = (hat2 * g2_ref[...] + s2_ref[...]).astype(BF16)
    grad_two = norm_back(dy_ref[...].astype(F32), hat2, inv2, g2_ref[...])
    acc[...] = grad_two
    low[...] = grad_two.astype(BF16)

    def back_down(j):
        gh = dot_t(low[...], down[cols_of(j)])
        hid[j % 2] = (gh * slope[:, cols_of(j)].astype(F32)).astype(BF16)

    def back_up(j):
        acc[...] += dot_t(hid[j % 2], up[:, cols_of(j)])

    for j in range(count + 1):
        if j < count:
            back_down(j)
        if j >= 1:
            back_up(j - 1)

    grad_one = norm_back(acc[...], hat_s[...], inv1, g1_ref[...])
    gone_ref[...] = grad_one
    gmix_ref[...] = dot_t(grad_one.astype(BF16), wo_ref[...]).astype(BF16)


def feed_forward(res, dy, up, down, ub, wo, db, g1, s1, g2, s2, tb=256, chunk=512):
    rows, width = res.shape
    ff = up.shape[1]
    block = pl.BlockSpec((tb, width), lambda i: (i, 0))
    hbm = pl.BlockSpec(memory_space=pl.ANY)
    return pl.pallas_call(
        functools.partial(ffn_kernel, chunk),
        grid=(rows // tb,),
        in_specs=[block, block, hbm, hbm] + [whole(a) for a in (ub, wo, db, g1, s1, g2, s2)],
        out_specs=[block] * 3,
        out_shape=[jax.ShapeDtypeStruct((rows, width), t) for t in (BF16, F32, BF16)],
        scratch_shapes=[
            pltpu.VMEM((width, ff), BF16),
            pltpu.VMEM((ff, width), BF16),
            pltpu.VMEM((2, tb, chunk), F32),
            pltpu.VMEM((2, tb, chunk), BF16),
            pltpu.VMEM((tb, ff), BF16),
            pltpu.VMEM((tb, width), BF16),
            pltpu.VMEM((tb, width), F32),
            pltpu.VMEM((tb, width), F32),
            pltpu.SemaphoreType.DMA((2, ff // chunk)),
        ],
        compiler_params=pltpu.CompilerParams(vmem_limit_bytes=VMEM_LIMIT),
        name="feed_forward",
    )(res, dy, up, down, ub, wo, db, g1, s1, g2, s2)


def backward_kernel(group, p_ref, q_ref, k_ref, v_ref, mix_ref, do_ref, pk_ref, pv_ref, w_ref, gone_ref,
                    out_ref, gk_ref, gv_ref, kt, dk, dv, gj, delta, gbuf, dsbuf, dqt):
    step = pl.program_id(0)
    length = q_ref.shape[0]
    pre = pk_ref.shape[0]
    width = out_ref.shape[1]
    blocks = length // QB
    window = p_ref.shape[2] - pre
    ident = eye(QB)
    sub = lax.broadcasted_iota(jnp.int32, (8, PAIR), 0)
    lane = lax.broadcasted_iota(jnp.int32, (8, PAIR), 1)
    pick = jnp.where((sub == 0) == (lane < HEAD_DIM), 1.0, 0.0).astype(BF16)
    dk[...] = jnp.zeros_like(dk)
    dv[...] = jnp.zeros_like(dv)
    for g in range(group):
        cols = slice(g * PAIR, (g + 1) * PAIR)
        kt[cols, :length] = dot_t(ident, k_ref[:, cols]).astype(BF16)
        kt[cols, length:] = dot_t(ident, pk_ref[:, cols]).astype(BF16)
        prod = do_ref[:, cols].astype(F32) * mix_ref[:, cols].astype(F32)
        high = prod.astype(BF16)
        low = (prod - high.astype(F32)).astype(BF16)
        delta[g] = dot_t(pick, high) + dot_t(pick, low)

    def where_of(i):
        g, qb = divmod(i, blocks)
        start = min(max(qb * QB - QB, 0), length - window)
        return g, qb, slice(start, start + window), slice(qb * QB, (qb + 1) * QB), slice(g * PAIR, (g + 1) * PAIR)

    def grad_probs(i):
        g, qb, win, rows, cols = where_of(i)
        vals = jnp.concatenate([v_ref[win, cols], pv_ref[:, cols]], axis=0)
        gbuf[i % 2] = dot_t(vals, split_heads(do_ref[rows, cols]))

    def grad_scores(i):
        g, qb, win, rows, cols = where_of(i)
        d = jnp.concatenate([delta[g, 0:1, rows], delta[g, 1:2, rows]], axis=1)
        dsbuf[i % 2] = (p_ref[qb, g].astype(F32) * (gbuf[i % 2] - d)).astype(BF16)

    def grads(i):
        g, qb, win, rows, cols = where_of(i)
        ds = dsbuf[i % 2]
        dva = dot(p_ref[qb, g], split_heads(do_ref[rows, cols]))
        dv[win, cols] += dva[:window]
        dv[length:, cols] += dva[window:]
        dka = dot(ds, split_heads(q_ref[rows, cols]))
        dk[win, cols] += dka[:window]
        dk[length:, cols] += dka[window:]
        keys = jnp.concatenate([kt[cols, win], kt[cols, length:]], axis=1)
        dqt[cols, rows] = own_blocks(dot(keys, ds) * HEAD_DIM ** -0.5).astype(BF16)

    total = group * blocks
    for i in range(total + 2):
        if i < total:
            grad_probs(i)
        if 0 <= i - 1 < total:
            grad_scores(i - 1)
        if 0 <= i - 2 < total:
            grads(i - 2)
    gw = group * PAIR
    big = eye(256)
    for r in range(length // 256):
        rr = slice(r * 256, (r + 1) * 256)
        gj[step, rr, 0:gw] = dot_t(big, dqt[:, rr]).astype(BF16)
    gj[step, :, gw:2 * gw] = dk[:length].astype(BF16)
    gj[step, :, 2 * gw:] = dv[:length].astype(BF16)
    gk_ref[...] = dk[length:]
    gv_ref[...] = dv[length:]

    @pl.when(step == pl.num_programs(0) - 1)
    def _():
        steps = width // gw
        for r in range(length // 256):
            rr = slice(r * 256, (r + 1) * 256)
            acc = gone_ref[rr]
            for part in range(3):
                x = jnp.concatenate([gj[i, rr, part * gw:(part + 1) * gw] for i in range(steps)], axis=1)
                acc = acc + dot_t(x, w_ref[:, part * width:(part + 1) * width])
            out_ref[rr] = acc.astype(BF16)


def attend_backward(p, q, k, v, mix, do, pk, pv, wqkv, gone, group=2):
    length, width = q.shape
    pre = pk.shape[0]
    blocks, pairs, depth, _ = p.shape
    gw = group * PAIR

    def col(a):
        return pl.BlockSpec((a.shape[0], gw), lambda i: (0, i))

    out_spec, out_shape = kept((length, width), BF16)
    return pl.pallas_call(
        functools.partial(backward_kernel, group),
        grid=(pairs // group,),
        in_specs=[pl.BlockSpec((blocks, group, depth, 2 * QB), lambda i: (0, i, 0, 0))]
        + [col(a) for a in (q, k, v, mix, do, pk, pv)] + [whole(wqkv), whole(gone)],
        out_specs=[out_spec, col(pk), col(pv)],
        out_shape=[out_shape] + [jax.ShapeDtypeStruct((pre, width), F32)] * 2,
        scratch_shapes=[
            pltpu.VMEM((gw, length + pre), BF16),
            pltpu.VMEM((length + pre, gw), F32),
            pltpu.VMEM((length + pre, gw), F32),
            pltpu.VMEM((pairs // group, length, 3 * gw), BF16),
            pltpu.VMEM((group, 8, length), F32),
            pltpu.VMEM((2, depth, 2 * QB), F32),
            pltpu.VMEM((2, depth, 2 * QB), BF16),
            pltpu.VMEM((gw, length), BF16),
        ],
        compiler_params=pltpu.CompilerParams(vmem_limit_bytes=VMEM_LIMIT),
        name="attend_backward",
    )(p, q, k, v, mix, do, pk, pv, wqkv, gone)


def on_device(tokens, segment_ids, qkv_weight, prefix_keys, prefix_values, out_weight, out_bias, norm1_gain, norm1_shift,
              up_weight, up_bias, down_weight, down_bias, norm2_gain, norm2_shift, out_grad):
    row = lambda a: a.reshape(1, -1)
    up_all = lax.all_gather(up_weight, "mp", axis=1, tiled=True)
    down_all = lax.all_gather(down_weight, "mp", axis=0, tiled=True)
    bias_all = lax.all_gather(up_bias, "mp", axis=0, tiled=True)
    q, k, v, mix, probs, res = attend_forward(
        tokens[0], qkv_weight, segment_ids, prefix_keys, prefix_values, out_weight, row(out_bias))
    out, grad_one, grad_mixed = feed_forward(
        res, out_grad[0], up_all, down_all, row(bias_all), out_weight, row(down_bias), row(norm1_gain), row(norm1_shift),
        row(norm2_gain), row(norm2_shift))
    grad_tokens, gk, gv = attend_backward(
        probs, q, k, v, mix, grad_mixed, prefix_keys, prefix_values, qkv_weight, grad_one)
    total_k, total_v = lax.psum((gk, gv), ("dp", "mp"))
    return out[None], grad_tokens[None], total_k, total_v


def solution(mesh):
    rows = P(("dp", "mp"), None, None)
    return jax.shard_map(
        on_device,
        mesh=mesh,
        in_specs=(rows, P(("dp", "mp"), None), P(), P(), P(), P(), P(), P(), P(), P(None, "mp"), P("mp"), P("mp", None),
                  P(), P(), P(), rows),
        out_specs=(rows, rows, P(), P()),
        check_vma=False,
    )
```

time: 659 us -> 387 us (0.59)
  matrix products: 338 us -> 0 us
  Pallas kernels: 0 us -> 121 us
  waiting for transfers between devices: 106 us -> 224 us
  other arithmetic: 101 us -> 0 us
  local copies, waits for them, and re-layouts: 63.2 us -> 4 us
  loops' own time: 7.31 us -> 0 us
    dot_general x22 -> x0, matrix products: 338 us -> none  [the longest x4 87.4 us: block_scores(): jnp.einsum('qhd,khd->hqk', query_block, keys_all, preferred_element_type=...]
    pallas_call x0 -> x3, Pallas kernels: none -> 121 us  [the longest x1 52.7 us: feed_forward(): pl.pallas_call(functools.partial(ffn_kernel, chunk), grid=(rows // tb,),...]
    all_gather x2, waiting for transfers between devices: 0.02 us -> 96.1 us  [the longest x1 75.3 us: on_device(): down_all = lax.all_gather(down_weight, 'mp', axis=0, tiled=True)]
    convert_element_type x3 -> x0, other arithmetic: 59.4 us -> none  [the longest x2 58.8 us: one_block(): grad_scores = (probs * (grad_probs - delta)).astype(jnp.bfloat16)]
    reduce_sum x5 -> x0, other arithmetic: 37.8 us -> none  [the longest x2 30.5 us: one_block(): total = jnp.sum(expo, -1, keepdims=True)]
    psum x1, waiting for transfers between devices: 104 us -> 127 us  [on_device(): total_k, total_v = lax.psum((gk, gv), ('dp', 'mp'))]
    unnamed x62 -> x3, local copies, waits for them, and re-layouts: 23.8 us -> 4 us
    slice x8 -> x0, local copies, waits for them, and re-layouts: 16 us -> none  [the longest x1 4.69 us: attend_backward(): grad_keys[PRE:]]
  transfers between devices with their start and end apart: 3 -> 3, of which waited for: 1 -> 3; matrix products, arithmetic and copies ran while one was open for 28% -> 0% of each run, Pallas kernels for 0% -> 10%
where the time goes in v1:
time: 387 us
  waiting for transfers between devices  224 us (58%)
  Pallas kernels  121 us (31%)
  blocking collectives  24 us (6%)
  between operations  13.8 us (4%)
  local copies, waits for them, and re-layouts  4 us (1%)
    psum x1, waiting for transfers between devices, on_device(): total_k, total_v = lax.psum((gk, gv), ('dp', 'mp'))  127 us
    all_gather x1, waiting for transfers between devices, on_device(): down_all = lax.all_gather(down_weight, 'mp', axis=0, tiled=True)  75.3 us
    pallas_call x1, Pallas kernels, feed_forward(): pl.pallas_call(functools.partial(ffn_kernel, chunk), grid=(rows // tb,),...  52.7 us
    pallas_call x1, Pallas kernels, attend_forward(): pl.pallas_call(forward_kernel, grid=(blocks,), in_specs=[whole(a) for a i...  36.9 us
    pallas_call x1, Pallas kernels, attend_backward(): pl.pallas_call(functools.partial(backward_kernel, group), grid=(pairs //...  31.5 us
    all_gather x1, blocking collectives, on_device(): bias_all = lax.all_gather(up_bias, 'mp', axis=0, tiled=True)  24 us
    all_gather x1, waiting for transfers between devices, on_device(): up_all = lax.all_gather(up_weight, 'mp', axis=1, tiled=True)  20.9 us
  transfers between devices with their start and end apart: 3, of which 3 were waited for; matrix products, arithmetic and copies ran while one was open for 0% of the time, Pallas kernels for 10%

profile of v1, /device:TPU:0, one launch (start us, length us, event | category | flops | bytes accessed | tf_op | source)
XLA Modules:
  0.0 387.1 jit_solution(4862666091027030709)
XLA Ops:
  7.2 0.0 all-gather.4.cloned.1.call-start
  7.2 0.7 all-gather.4.cloned.1.call-update
  7.9 0.0 all-gather.6.cloned.1.call-start
  7.9 0.7 all-gather.6.cloned.1.call-update
  8.6 0.0 all-reduce.3.cloned.1.call-start
  8.7 0.7 reshape.36
  9.4 36.9 %attend_forward.1 = (bf16[1024,1024]{1,0:T(8,128)(2,1)}, bf16[1024,1024]{1,0:T(8,128)(2,1)}, bf16[1024,1024]{1,0:T(8,128)(2,1)}, bf16[1024,1024]{1,0:T(8,128)(2,...) custom-call(bf16[1024,1024]{1,0:T(8,128)(2,1)} %bitcast.11, bf16[1024,3072]{1,0:T(8,128)(2,1)} %w_ref.1, ...), custom_call_target="tpu_custom_call" | custom-call | tf_op jit(solution)/shard_map/attend_forward/pallas_call | solution.py:152
  46.3 24.0 %all-gather = bf16[16,1,256]{2,1,0:T(2,128)(2,1)} all-gather(bf16[1,1,256]{2,1,0:T(2,128)(2,1)S(1)} %reshape.36), channel_id=1, replica_groups=mesh['dp'=2,'mp'=16] {'mp'}, dimensions={0}, use_global_device_ids=true | all-gather | bytes 8704 | tf_op jit(solution)/shard_map/all_gather | solution.py:388
  70.3 20.9 %all-gather.4.cloned.1.call-done.up_hbm = bf16[1024,4096]{1,0:T(8,128)(2,1)} async-done(((bf16[1024,256]{1,0:T(8,128)(2,1)}), bf16[1024,4096]{1,0:T(8,128)(2,1)}) %all-gather.4.cloned.1.call-update) | async-done | bytes 8388624 | tf_op jit(solution)/shard_map/all_gather | solution.py:386
  91.2 75.3 %all-gather.6.cloned.1.call-done.down_hbm = bf16[4096,1024]{1,0:T(8,128)(2,1)} async-done(((bf16[256,1024]{1,0:T(8,128)(2,1)}), bf16[4096,1024]{1,0:T(8,128)(2,1)}) %all-gather.6.cloned.1.call-update) | async-done | bytes 8388624 | tf_op jit(solution)/shard_map/all_gather | solution.py:387
  166.4 52.7 %feed_forward.1 = (bf16[1024,1024]{1,0:T(8,128)(2,1)}, f32[1024,1024]{1,0:T(8,128)}, bf16[1024,1024]{1,0:T(8,128)(2,1)}) custom-call(f32[1024,1024]{1,0:T(8,128)} %get-tuple-element.16.res_ref, bf16[1024,1024]{1,0:T(8,128)(2,1)} %bitcast.12, bf16[1024,4096]{1,0:T(8,128)(2,1)} %all-gather.4.cloned.1.call-done.up_hbm, ...), custom_call_target="tpu_custom_call" | custom-call | tf_op jit(solution)/shard_map/feed_forward/pallas_call | solution.py:249
  219.1 31.5 %attend_backward.1 = (bf16[1024,1024]{1,0:T(8,128)(2,1)}, f32[64,1024]{1,0:T(8,128)}, f32[64,1024]{1,0:T(8,128)}) custom-call(bf16[8,8,448,256]{3,2,1,0:T(8,128)(2,1)} %get-tuple-element.18.p_ref, bf16[1024,1024]{1,0:T(8,128)(2,1)} %get-tuple-element.19.q_ref, bf16[1024,1024]{1,0:T(8,128)(2,1)} %get-tuple-element.20.k_ref, ...), custom_call_target="tpu_custom_call" | custom-call | tf_op jit(solution)/shard_map/attend_backward/pallas_call | solution.py:361
  250.6 0.0 all-reduce.3.cloned.1.call-update
  250.6 126.6 %all-reduce.3.cloned.1.call-done = (f32[64,1024]{1,0:T(8,128)}, f32[64,1024]{1,0:T(8,128)}) async-done(((f32[64,1024]{1,0:T(8,128)}, f32[64,1024]{1,0:T(8,128)}), (f32[64,1024]{1,0:T(8,128)}, f32[64,1024]{1,0:T(8,128)})) %all-reduce.3.cloned.1.call-update) | async-done | bytes 524304 | tf_op jit(solution)/shard_map/psum | solution.py:396
  377.2 1.7 copy.22
  378.9 1.7 copy.23
Async XLA Ops:
  7.2 84.0 %all-gather.4.cloned.1.call-start = ((), (), s32[]{:S(2)}) async-start(), calls=%async_computation | async-start | bytes 8912896 | tf_op jit(solution)/shard_map/all_gather | solution.py:386
  7.9 158.5 %all-gather.6.cloned.1.call-start = ((), (), s32[]{:S(2)}) async-start(), calls=%async_computation.1 | async-start | bytes 8912896 | tf_op jit(solution)/shard_map/all_gather | solution.py:387
  8.6 368.6 %all-reduce.3.cloned.1.call-start = ((), (), s32[]{:S(2)}) async-start(), calls=%async_computation.2 | async-start | bytes 1048576 | tf_op jit(solution)/shard_map/psum | solution.py:396
Sparse Core Ops, SparseCore 0:
  10.2 80.9 all-gather.3
  93.3 73.0 all-gather.5
  250.8 126.3 all-reduce.2

commit v2 on v1

--- a/solution.py
+++ b/solution.py
@@ -17,6 +17,8 @@
 F32 = jnp.float32
 BF16 = jnp.bfloat16
 VMEM_LIMIT = 62 * 1024 * 1024
+BIAS_ROWS = 32
+GATHER_SLOTS = ((0, 0, 0), (1, 1, 0), (2, 0, 1), (4, 1, 1), (5, 0, 2), (7, 1, 2), (8, 0, 3), (9, 1, 3), (9, 0, 4), (9, 1, 4))
 
 
 def dot(a, b):
@@ -67,16 +69,216 @@
     return spec, jax.ShapeDtypeStruct(shape, dtype)
 
 
-def forward_kernel(tok_ref, wqkv_ref, seg_ref, pk_ref, pv_ref, wo_ref, bo_ref,
-                   q_out, k_out, v_out, mix_out, p_out, res_out,
-                   vt, pvt, segc, bias, sbuf, mixt):
+LINE = 4
+
+
+def flip(x, bits):
+    bit = 1
+    while bit <= bits:
+        if bits & bit:
+            x = x + bit - 2 * bit * ((x // bit) % 2)
+        bit *= 2
+    return x
+
+
+def guarded(condition, body):
+    if condition is None:
+        body()
+    else:
+        pl.when(condition)(body)
+
+
+def gather_keys(count_b):
+    others = range(1, count_b)
+    keys = [("z", side, d, 0) for side in (1, -1) for d in (1, 2, 3)]
+    keys += [("z", side, d, 1) for side in (1, -1) for d in (1, 2)]
+    for s in others:
+        keys += [("x", s, d, 0) for d in (0, 1, -1, 2, 3)] + [("x", s, 3, 1)]
+        keys += [("y", s, d, 0) for d in (0, 1, -1, 2)]
+    keys.append(("y", 0, 3, 0))
+    keys.append(("core", 0, 0, None))
+    for s in range(count_b):
+        keys += [("core", s, d, part) for d in (0, 1, -1, 2, 3) for part in (0, 1) if (s, d) != (0, 0)]
+    return {key: i for i, key in enumerate(keys)}
+
+
+def gather_events(count_b):
+    others = range(1, count_b)
+    sides = (1, -1)
+    return [
+        [("x", s, 0, 0) for s in others] + [("z", side, 1, 0) for side in sides],
+        [("z", side, 2, 0) for side in sides] + [("x", s, d, 0) for s in others for d in sides] + [("y", s, 0, 0) for s in others],
+        [("z", side, 3, 0) for side in sides] + [("x", s, 2, 0) for s in others] + [("z", side, 1, 1) for side in sides]
+        + [("y", s, d, 0) for s in others for d in sides],
+        [("y", 0, 3, 0)] + [("x", s, 3, 0) for s in others] + [("z", side, 2, 1) for side in sides],
+        [("y", s, 2, 0) for s in others] + [("x", s, 3, 1) for s in others],
+    ]
+
+
+class Gather:
+    def __init__(self, count_b, inputs, alls, sems):
+        self.count_b = count_b
+        self.inputs, self.alls = inputs, alls
+        self.send, self.recv = sems
+        self.dp = lax.axis_index("dp")
+        self.mp = lax.axis_index("mp")
+        self.core = self.mp % 2
+        self.b = (self.mp // 2) % self.count_b
+        self.a = self.mp // (2 * self.count_b)
+        self.half = self.dp % 2
+        self.keys = gather_keys(count_b)
+
+    def index(self, a, s, other=False):
+        core = 1 - self.core if other else self.core
+        return (a * self.count_b + flip(self.b, s)) * 2 + core
+
+    def at(self, d):
+        if d in (2, 3):
+            return self.a + d - 2 * d * ((self.a + d) // LINE)
+        return self.a + d
+
+    def inside(self, d):
+        if d == 1:
+            return self.a < LINE - 1
+        if d == -1:
+            return self.a > 0
+        if d == 3:
+            return self.a % 3 == 0
+        return None
+
+    def gets(self, key):
+        kind, s, d, part = key
+        if kind != "z":
+            return self.inside(d)
+        return self.a + d < LINE if s == 1 else self.a >= d
+
+    def sends(self, key):
+        kind, s, d, part = key
+        if kind != "z":
+            return self.inside(d)
+        low, high = (1, LINE - d) if s == 1 else (d - 1, LINE - 2)
+        return (self.a >= low) & (self.a <= high)
+
+    def copy(self, t, key, arriving):
+        kind, s, d, part = key
+        own = d == 0 and not arriving
+        if kind == "z":
+            own = d == 1 and not arriving
+            target = (self.dp, self.index(self.a - s, 0))
+            chunk = self.index(self.a + s * d, 0) if arriving else self.index(self.a + s * (d - 1), 0)
+        elif kind == "x":
+            target = (self.dp, self.index(self.a, s))
+            chunk = self.index(self.at(d), s if arriving else 0)
+        elif kind == "y":
+            target = (flip(self.dp, 1), self.mp)
+            chunk = self.index(self.at(d), s)
+            own = False
+        else:
+            target = (self.dp, self.index(self.a, 0, True))
+            chunk = self.index(self.at(d), s, arriving)
+            own = own and s == 0
+        ref = self.alls[t]
+        rows = ref.shape[1]
+        if part is None:
+            span = pl.ds(0, rows)
+        else:
+            which = 1 - part if kind == "y" and arriving else part
+            which = self.half if which == 0 else 1 - self.half
+            span = pl.ds(pl.multiple_of(which * (rows // 2), 16), rows // 2)
+        src = self.inputs[t].at[span] if own else ref.at[chunk, span]
+        number = self.keys[key]
+        return pltpu.make_async_remote_copy(
+            src_ref=src, dst_ref=ref.at[chunk, span], send_sem=self.send.at[t, number], recv_sem=self.recv.at[t, number],
+            device_id=target, device_id_type=pl.DeviceIdType.MESH)
+
+    def start(self, t, *key):
+        guarded(self.sends(key), lambda: self.copy(t, key, False).start())
+
+    def arrive(self, t, key):
+        self.copy(t, key, True).wait_recv()
+
+    def greet(self):
+        barrier = pltpu.get_barrier_semaphore()
+        partners = [(self.inside(d), (self.dp, self.index(self.a + d, 0))) for d in (1, -1)]
+        partners += [(None, (self.dp, self.index(self.a, s))) for s in range(1, self.count_b)]
+        partners += [(None, (self.dp, self.index(self.a, 0, True))), (None, (flip(self.dp, 1), self.mp))]
+        for condition, device in partners:
+            guarded(condition, lambda: pl.semaphore_signal(
+                barrier, inc=1, device_id=device, device_id_type=pl.DeviceIdType.MESH))
+        ends = 1 - (self.a % 3 + 1) // 2
+        pl.semaphore_wait(barrier, len(partners) - ends)
+
+    def open(self, t):
+        for side in (1, -1):
+            self.start(t, "z", side, 1, 0)
+        for s in range(1, self.count_b):
+            self.start(t, "x", s, 0, 0)
+        self.start(t, "core", 0, 0, None)
+
+    def pass_on(self, t, key):
+        kind, s, d, part = key
+
+        def body():
+            self.arrive(t, key)
+            if kind == "z":
+                if d < (3 if part == 0 else 2):
+                    self.start(t, "z", s, d + 1, part)
+                at = s if d == 1 else d
+                if part == 0:
+                    for other in range(1, self.count_b):
+                        self.start(t, "x", other, at, 0)
+                    if d == 3:
+                        self.start(t, "y", 0, 3, 0)
+                self.start(t, "core", 0, at, part)
+            elif kind == "x":
+                if d != 3:
+                    self.start(t, "y", s, d, 0)
+                self.start(t, "core", s, d, part)
+            else:
+                if d == 3:
+                    for other in range(1, self.count_b):
+                        self.start(t, "x", other, 3, 1)
+                self.start(t, "core", s, d, 1)
+
+        guarded(self.gets(key), body)
+
+    def level(self, t, n):
+        for key in gather_events(self.count_b)[n]:
+            self.pass_on(t, key)
+        if n == 0:
+            for side in (1, -1):
+                self.start(t, "z", side, 1, 1)
+
+    def finish(self, t):
+        for key in self.keys:
+            if key[0] == "core":
+                guarded(self.gets(key), lambda: self.arrive(t, key))
+
+    def close(self, t):
+        for key in self.keys:
+            guarded(self.sends(key), lambda: self.copy(t, key, False).wait_send())
+
+
+def forward_kernel(count_b, tok_ref, wqkv_ref, seg_ref, pk_ref, pv_ref, wo_ref, bo_ref, up_in, down_in,
+                   q_out, k_out, v_out, mix_out, p_out, res_out, up_all, down_all,
+                   vt, pvt, segc, bias, sbuf, mixt, send, recv):
     qb = pl.program_id(0)
+    gather = Gather(count_b, (up_in, down_in), (up_all, down_all), (send, recv))
+
+    def pass_on(now):
+        for slot, t, n in GATHER_SLOTS:
+            if slot == now:
+                gather.level(t, n)
+
     length, width = tok_ref.shape
     window = bias.shape[0]
     pairs = width // PAIR
 
     @pl.when(qb == 0)
     def _():
+        gather.greet()
+        gather.open(0)
+        gather.open(1)
         tile = 256
         for part, ref in enumerate((q_out, k_out, v_out)):
             for j in range(width // tile):
@@ -84,6 +286,8 @@
                 if part == 0:
                     x = x * jnp.asarray(HEAD_DIM ** -0.5, BF16)
                 ref[:, j * tile:(j + 1) * tile] = x
+                if part == 2 and j == 2:
+                    pass_on(0)
         big = eye(256)
         for j in range(width // 256):
             cols = slice(j * 256, (j + 1) * 256)
@@ -93,6 +297,12 @@
         seg = jnp.broadcast_to(seg_ref[...].astype(F32), (QB, length)).astype(BF16)
         for j in range(length // QB):
             segc[j * QB:(j + 1) * QB, :] = dot_t(ident, seg[:, j * QB:(j + 1) * QB])
+
+    for slot in range(1, length // QB):
+
+        @pl.when(qb == slot)
+        def _():
+            pass_on(slot)
 
     start = pl.multiple_of(jnp.clip(qb * QB - QB, 0, length - window), QB)
     win = pl.ds(start, window)
@@ -131,6 +341,7 @@
 
     @pl.when(qb == pl.num_programs(0) - 1)
     def _():
+        pass_on(8)
         big = eye(256)
         for r in range(length // 256):
             rr = slice(r * 256, (r + 1) * 256)
@@ -138,9 +349,14 @@
         for r in range(length // 256):
             rr = slice(r * 256, (r + 1) * 256)
             res_out[rr] = tok_ref[rr].astype(F32) + dot(mix_out[rr], wo_ref[...]) + bo_ref[...]
-
-
-def attend_forward(tok, wqkv, seg, pk, pv, wo, bo):
+        pass_on(9)
+        for t in range(2):
+            gather.finish(t)
+        for t in range(2):
+            gather.close(t)
+
+
+def attend_forward(tok, wqkv, seg, pk, pv, wo, bo, up, down, group):
     length, width = tok.shape
     pre = pk.shape[0]
     window = 3 * QB
@@ -149,10 +365,14 @@
         (pl.BlockSpec((1, pairs, window + pre, 2 * QB), lambda i: (i, 0, 0, 0)),
          jax.ShapeDtypeStruct((blocks, pairs, window + pre, 2 * QB), BF16)),
         kept((length, width), F32)]
+    hbm = pl.BlockSpec(memory_space=pl.ANY)
+    outs += [(hbm, jax.ShapeDtypeStruct((group,) + a.shape, BF16)) for a in (up, down)]
+    count_b = group // (2 * LINE)
+    pieces = len(gather_keys(count_b))
     return pl.pallas_call(
-        forward_kernel,
+        functools.partial(forward_kernel, count_b),
         grid=(blocks,),
-        in_specs=[whole(a) for a in (tok, wqkv, seg, pk, pv, wo, bo)],
+        in_specs=[whole(a) for a in (tok, wqkv, seg, pk, pv, wo, bo)] + [hbm, hbm],
         out_specs=[o[0] for o in outs],
         out_shape=[o[1] for o in outs],
         scratch_shapes=[
@@ -162,37 +382,46 @@
             pltpu.VMEM((window, QB), F32),
             pltpu.VMEM((2, window + pre, 2 * QB), F32),
             pltpu.VMEM((width, length), BF16),
+            pltpu.SemaphoreType.DMA((2, pieces)),
+            pltpu.SemaphoreType.DMA((2, pieces)),
         ],
-        compiler_params=pltpu.CompilerParams(vmem_limit_bytes=VMEM_LIMIT),
+        compiler_params=pltpu.CompilerParams(vmem_limit_bytes=VMEM_LIMIT, collective_id=0, has_side_effects=True),
         name="attend_forward",
-    )(tok, wqkv, seg, pk, pv, wo, bo)
-
-
-def ffn_kernel(chunk, res_ref, dy_ref, up_hbm, down_hbm, ub_ref, wo_ref, db_ref, g1_ref, s1_ref, g2_ref, s2_ref,
-               out_ref, gone_ref, gmix_ref, up, down, pre, hid, slope, low, acc, hat_s, sems):
+    )(tok, wqkv, seg, pk, pv, wo, bo, up, down)
+
+
+def ffn_kernel(chunk, res_ref, dy_ref, up_hbm, down_hbm, up_own, down_own, wo_ref, db_ref, g1_ref, s1_ref, g2_ref, s2_ref,
+               out_ref, gone_ref, gmix_ref, up, down, ub, pre, hid, slope, low, acc, hat_s, sems):
     step = pl.program_id(0)
     count = up.shape[1] // chunk
-
-    def fetch(j):
-        cols = pl.ds(j * chunk, chunk)
-        return (
-            pltpu.make_async_copy(up_hbm.at[:, cols], up.at[:, cols], sems.at[0, j]),
-            pltpu.make_async_copy(down_hbm.at[cols], down.at[cols], sems.at[1, j]),
-        )
+    width = up.shape[0]
+    parts, _, part = up_hbm.shape
+
+    me = lax.axis_index("mp")
+
+    def fetch(d, t):
+        cols = pl.ds(d * part, part)
+        up_src, down_src = (up_own, down_own) if d == 0 else (up_hbm.at[(me + d) % parts], down_hbm.at[(me + d) % parts])
+        src = (up_src.at[pl.ds(0, width)], up_src.at[pl.ds(width, BIAS_ROWS)], down_src)[t]
+        dst = (up.at[:, cols], ub.at[:, cols], down.at[cols])[t]
+        return pltpu.make_async_copy(src, dst, sems.at[t, d])
 
     @pl.when(step == 0)
     def _():
-        for j in range(count):
-            for copy in fetch(j):
-                copy.start()
-        for j in range(count):
-            for copy in fetch(j):
-                copy.wait()
+        for t in range(3):
+            for d in range(parts):
+                fetch(d, t).start()
 
     hat, inv1 = normalize(res_ref[...])
     hat_s[...] = hat
     low[...] = (hat * g1_ref[...] + s1_ref[...]).astype(BF16)
 
+    @pl.when(step == 0)
+    def _():
+        for t in range(2):
+            for d in range(parts):
+                fetch(d, t).wait()
+
     def cols_of(j):
         return slice(j * chunk, (j + 1) * chunk)
 
@@ -200,7 +429,7 @@
         pre[j % 2] = dot(low[...], up[:, cols_of(j)])
 
     def act(j):
-        u = pre[j % 2] + ub_ref[:, cols_of(j)].astype(F32)
+        u = pre[j % 2] + ub[0:1, cols_of(j)].astype(F32)
         half = 0.5 * lax.erf(u * ROOT_HALF) + 0.5
         hid[j % 2] = (u * half).astype(BF16)
         slope[:, cols_of(j)] = (half + u * (jnp.exp(-0.5 * u * u) * INV_ROOT_TWOPI)).astype(BF16)
@@ -210,6 +439,13 @@
 
     acc[...] = jnp.zeros_like(acc)
     for j in range(count + 2):
+        if j == 2:
+
+            @pl.when(step == 0)
+            def _():
+                for d in range(parts):
+                    fetch(d, 2).wait()
+
         if j < count:
             rows_up(j)
         if 0 <= j - 2 < count:
@@ -241,31 +477,33 @@
     gmix_ref[...] = dot_t(grad_one.astype(BF16), wo_ref[...]).astype(BF16)
 
 
-def feed_forward(res, dy, up, down, ub, wo, db, g1, s1, g2, s2, tb=256, chunk=512):
+def feed_forward(res, dy, up, down, up_own, down_own, wo, db, g1, s1, g2, s2, tb=256, chunk=512):
     rows, width = res.shape
-    ff = up.shape[1]
+    parts, ffl, _ = down.shape
+    ff = parts * ffl
     block = pl.BlockSpec((tb, width), lambda i: (i, 0))
     hbm = pl.BlockSpec(memory_space=pl.ANY)
     return pl.pallas_call(
         functools.partial(ffn_kernel, chunk),
         grid=(rows // tb,),
-        in_specs=[block, block, hbm, hbm] + [whole(a) for a in (ub, wo, db, g1, s1, g2, s2)],
+        in_specs=[block, block] + [hbm] * 4 + [whole(a) for a in (wo, db, g1, s1, g2, s2)],
         out_specs=[block] * 3,
         out_shape=[jax.ShapeDtypeStruct((rows, width), t) for t in (BF16, F32, BF16)],
         scratch_shapes=[
             pltpu.VMEM((width, ff), BF16),
             pltpu.VMEM((ff, width), BF16),
+            pltpu.VMEM((BIAS_ROWS, ff), BF16),
             pltpu.VMEM((2, tb, chunk), F32),
             pltpu.VMEM((2, tb, chunk), BF16),
             pltpu.VMEM((tb, ff), BF16),
             pltpu.VMEM((tb, width), BF16),
             pltpu.VMEM((tb, width), F32),
             pltpu.VMEM((tb, width), F32),
-            pltpu.SemaphoreType.DMA((2, ff // chunk)),
+            pltpu.SemaphoreType.DMA((3, parts)),
         ],
         compiler_params=pltpu.CompilerParams(vmem_limit_bytes=VMEM_LIMIT),
         name="feed_forward",
-    )(res, dy, up, down, ub, wo, db, g1, s1, g2, s2)
+    )(res, dy, up, down, up_own, down_own, wo, db, g1, s1, g2, s2)
 
 
 def backward_kernel(group, p_ref, q_ref, k_ref, v_ref, mix_ref, do_ref, pk_ref, pv_ref, w_ref, gone_ref,
@@ -380,16 +618,14 @@
     )(p, q, k, v, mix, do, pk, pv, wqkv, gone)
 
 
-def on_device(tokens, segment_ids, qkv_weight, prefix_keys, prefix_values, out_weight, out_bias, norm1_gain, norm1_shift,
-              up_weight, up_bias, down_weight, down_bias, norm2_gain, norm2_shift, out_grad):
+def on_device(group, tokens, segment_ids, qkv_weight, prefix_keys, prefix_values, out_weight, out_bias, norm1_gain,
+              norm1_shift, up_weight, up_bias, down_weight, down_bias, norm2_gain, norm2_shift, out_grad):
     row = lambda a: a.reshape(1, -1)
-    up_all = lax.all_gather(up_weight, "mp", axis=1, tiled=True)
-    down_all = lax.all_gather(down_weight, "mp", axis=0, tiled=True)
-    bias_all = lax.all_gather(up_bias, "mp", axis=0, tiled=True)
-    q, k, v, mix, probs, res = attend_forward(
-        tokens[0], qkv_weight, segment_ids, prefix_keys, prefix_values, out_weight, row(out_bias))
+    up_part = jnp.concatenate([up_weight, jnp.broadcast_to(row(up_bias), (BIAS_ROWS, up_bias.shape[0]))], axis=0)
+    q, k, v, mix, probs, res, up_all, down_all = attend_forward(
+        tokens[0], qkv_weight, segment_ids, prefix_keys, prefix_values, out_weight, row(out_bias), up_part, down_weight, group)
     out, grad_one, grad_mixed = feed_forward(
-        res, out_grad[0], up_all, down_all, row(bias_all), out_weight, row(down_bias), row(norm1_gain), row(norm1_shift),
+        res, out_grad[0], up_all, down_all, up_part, down_weight, out_weight, row(down_bias), row(norm1_gain), row(norm1_shift),
         row(norm2_gain), row(norm2_shift))
     grad_tokens, gk, gv = attend_backward(
         probs, q, k, v, mix, grad_mixed, prefix_keys, prefix_values, qkv_weight, grad_one)
@@ -400,7 +636,7 @@
 def solution(mesh):
     rows = P(("dp", "mp"), None, None)
     return jax.shard_map(
-        on_device,
+        functools.partial(on_device, mesh.shape["mp"]),
         mesh=mesh,
         in_specs=(rows, P(("dp", "mp"), None), P(), P(), P(), P(), P(), P(), P(), P(None, "mp"), P("mp"), P("mp", None),
                   P(), P(), P(), rows),

time: 387 us -> 320 us (0.83)
  waiting for transfers between devices: 224 us -> 127 us
  Pallas kernels: 121 us -> 173 us
  blocking collectives: 24 us -> 0 us
    all_gather x2 -> x0, waiting for transfers between devices: 96.1 us -> none  [the longest x1 75.3 us: on_device(): down_all = lax.all_gather(down_weight, 'mp', axis=0, tiled=True)]
    pallas_call x1, Pallas kernels: 36.9 us -> 85.6 us  [attend_forward(): pl.pallas_call(functools.partial(forward_kernel, count_b), grid=(blocks,)...]
    all_gather x1 -> x0, blocking collectives: 24 us -> none  [on_device(): bias_all = lax.all_gather(up_bias, 'mp', axis=0, tiled=True)]
  transfers between devices with their start and end apart: 3 -> 1, of which waited for: 3 -> 1; matrix products, arithmetic and copies ran while one was open for 0% -> 0% of each run, Pallas kernels for 10% -> 0%
where the time goes in v2:
time: 320 us
  Pallas kernels  173 us (54%)
  waiting for transfers between devices  127 us (40%)
  between operations  14 us (4%)
  local copies, waits for them, and re-layouts  4 us (1%)
    psum x1, waiting for transfers between devices, on_device(): total_k, total_v = lax.psum((gk, gv), ('dp', 'mp'))  127 us
    pallas_call x1, Pallas kernels, attend_forward(): pl.pallas_call(functools.partial(forward_kernel, count_b), grid=(blocks,)...  85.6 us
    pallas_call x1, Pallas kernels, feed_forward(): pl.pallas_call(functools.partial(ffn_kernel, chunk), grid=(rows // tb,),...  56.2 us
    pallas_call x1, Pallas kernels, attend_backward(): pl.pallas_call(functools.partial(backward_kernel, group), grid=(pairs //...  31.5 us
  transfers between devices with their start and end apart: 1, of which 1 were waited for; matrix products, arithmetic and copies ran while one was open for 0% of the time, Pallas kernels for 0%

profile of v2, /device:TPU:0, one launch (start us, length us, event | category | flops | bytes accessed | tf_op | source)
XLA Modules:
  0.0 319.9 jit_solution(8692199522078815312)
XLA Ops:
  7.2 0.0 all-reduce.3.cloned.1.call-start
  7.2 0.7 broadcast_in_dim.11
  7.9 1.9 pad_maximum_fusion.up_in.up_own
  9.7 85.6 %attend_forward.1 = (bf16[1024,1024]{1,0:T(8,128)(2,1)}, bf16[1024,1024]{1,0:T(8,128)(2,1)}, bf16[1024,1024]{1,0:T(8,128)(2,1)}, bf16[1024,1024]{1,0:T(8,128)(2,...) custom-call(bf16[1024,1024]{1,0:T(8,128)(2,1)} %bitcast.10, ...), custom_call_target="tpu_custom_call" | custom-call | tf_op jit(solution)/shard_map/attend_forward/pallas_call | solution.py:372
  95.3 56.2 %feed_forward.1 = (bf16[1024,1024]{1,0:T(8,128)(2,1)}, f32[1024,1024]{1,0:T(8,128)}, bf16[1024,1024]{1,0:T(8,128)(2,1)}) custom-call(f32[1024,1024]{1,0:T(8,128)} %get-tuple-element.18.res_ref, bf16[1024,1024]{1,0:T(8,128)(2,1)} %bitcast.11, bf16[16,1056,256]{2,1,0:T(8,128)(2,1)} %get-tuple-element.19.up_hbm, ...), custom_call_target="tpu_custom_call" | custom-call | tf_op jit(solution)/shard_map/feed_forward/pallas_call | solution.py:486
  151.5 31.5 %attend_backward.1 = (bf16[1024,1024]{1,0:T(8,128)(2,1)}, f32[64,1024]{1,0:T(8,128)}, f32[64,1024]{1,0:T(8,128)}) custom-call(bf16[8,8,448,256]{3,2,1,0:T(8,128)(2,1)} %get-tuple-element.22.p_ref, bf16[1024,1024]{1,0:T(8,128)(2,1)} %get-tuple-element.23.q_ref, bf16[1024,1024]{1,0:T(8,128)(2,1)} %get-tuple-element.24.k_ref, ...), custom_call_target="tpu_custom_call" | custom-call | tf_op jit(solution)/shard_map/attend_backward/pallas_call | solution.py:599
  183.0 0.0 all-reduce.3.cloned.1.call-update
  183.0 126.7 %all-reduce.3.cloned.1.call-done = (f32[64,1024]{1,0:T(8,128)}, f32[64,1024]{1,0:T(8,128)}) async-done(((f32[64,1024]{1,0:T(8,128)}, f32[64,1024]{1,0:T(8,128)}), (f32[64,1024]{1,0:T(8,128)}, f32[64,1024]{1,0:T(8,128)})) %all-reduce.3.cloned.1.call-update) | async-done | bytes 524304 | tf_op jit(solution)/shard_map/psum | solution.py:632
  309.7 1.7 copy.22
  311.4 1.7 copy.23
Async XLA Ops:
  7.2 302.5 %all-reduce.3.cloned.1.call-start = ((), (), s32[]{:S(2)}) async-start(), calls=%async_computation | async-start | bytes 1048576 | tf_op jit(solution)/shard_map/psum | solution.py:632
Sparse Core Ops, SparseCore 0:
  183.2 126.4 all-reduce.2

commit v3 on v2

--- a/solution.py
+++ b/solution.py
@@ -506,137 +506,237 @@
     )(res, dy, up, down, up_own, down_own, wo, db, g1, s1, g2, s2)
 
 
-def backward_kernel(group, p_ref, q_ref, k_ref, v_ref, mix_ref, do_ref, pk_ref, pv_ref, w_ref, gone_ref,
-                    out_ref, gk_ref, gv_ref, kt, dk, dv, gj, delta, gbuf, dsbuf, dqt):
-    step = pl.program_id(0)
+class Total:
+    def __init__(self, count_dp, count_mp, low, slots, parts, result, sems):
+        self.low, self.slots, self.parts, self.result = low, slots, parts, result
+        self.sems = sems
+        self.count_b = count_mp // (2 * LINE)
+        self.high_b, self.high_dp = self.count_b // 2, count_dp // 2
+        self.count_q = LINE * self.high_b * self.high_dp
+        dp, mp = lax.axis_index("dp"), lax.axis_index("mp")
+        b = (mp // 2) % self.count_b
+        a = mp // (2 * self.count_b)
+        self.g = ((dp % 2) * 2 + b % 2) * 2 + mp % 2
+        self.q = (a * self.high_b + b // 2) * self.high_dp + dp // 2
+
+    def device(self, g, q):
+        a, high = q // (self.high_b * self.high_dp), q % (self.high_b * self.high_dp)
+        dp = (high % self.high_dp) * 2 + g // 4
+        b = (high // self.high_dp) * 2 + (g // 2) % 2
+        return dp, (a * self.count_b + b) * 2 + g % 2
+
+    def near(self, j):
+        return self.device((self.g + j) % 8, self.q)
+
+    def far(self, i):
+        return self.device(self.g, (self.q + i) % self.count_q)
+
+    def copy(self, phase, j, arriving=False):
+        if phase == 0:
+            src, dst, to = self.low.at[(self.g + j) % 8], self.slots.at[j], self.near(j)
+        elif phase == 1:
+            at = (self.q + self.count_q - j) % self.count_q if arriving else self.q
+            src, dst, to = self.parts.at[at], self.parts.at[at], self.far(j)
+        else:
+            at = (self.g + 8 - j) % 8 if arriving else self.g
+            src, dst, to = self.result.at[at], self.result.at[at], self.near(j)
+        send, recv = self.sems[phase]
+        return pltpu.make_async_remote_copy(
+            src_ref=src, dst_ref=dst, send_sem=send.at[j], recv_sem=recv.at[j], device_id=to,
+            device_id_type=pl.DeviceIdType.MESH)
+
+    def peers(self, phase):
+        return range(1, self.count_q if phase == 1 else 8)
+
+    def greet(self):
+        barrier = pltpu.get_barrier_semaphore()
+        partners = [self.near(j) for j in self.peers(0)] + [self.far(i) for i in self.peers(1)]
+        for device in partners:
+            pl.semaphore_signal(barrier, inc=1, device_id=device, device_id_type=pl.DeviceIdType.MESH)
+        pl.semaphore_wait(barrier, len(partners))
+
+    def start(self, phase):
+        for j in self.peers(phase):
+            self.copy(phase, j).start()
+
+    def arrive(self, phase):
+        for j in self.peers(phase):
+            self.copy(phase, j, True).wait_recv()
+
+    def first(self):
+        self.greet()
+        self.start(0)
+
+    def second(self):
+        self.arrive(0)
+        total = self.low[self.g].astype(F32)
+        for j in self.peers(0):
+            total = total + self.slots[j].astype(F32)
+        self.parts[self.q] = total.astype(BF16)
+        self.start(1)
+
+    def third(self):
+        self.arrive(1)
+        total = self.parts[0].astype(F32)
+        for i in range(1, self.count_q):
+            total = total + self.parts[i].astype(F32)
+        self.result[self.g] = total.astype(BF16)
+        self.start(2)
+
+    def last(self):
+        self.arrive(2)
+        for phase in range(3):
+            for j in self.peers(phase):
+                self.copy(phase, j).wait_send()
+
+
+def backward_kernel(counts, p_ref, q_ref, k_ref, v_ref, mix_ref, do_ref, pk_ref, pv_ref, w_ref, gone_ref,
+                    out_ref, gk_ref, gv_ref, kt, dk, dv, gj, delta, gbuf, ds_all, dqt, low, slots, parts, result,
+                    send0, recv0, send1, recv1, send2, recv2):
+    pair = pl.program_id(0)
     length = q_ref.shape[0]
     pre = pk_ref.shape[0]
-    width = out_ref.shape[1]
+    pairs, width = ds_all.shape[0], out_ref.shape[1]
     blocks = length // QB
-    window = p_ref.shape[2] - pre
+    depth = p_ref.shape[2]
+    window = depth - pre
     ident = eye(QB)
     sub = lax.broadcasted_iota(jnp.int32, (8, PAIR), 0)
     lane = lax.broadcasted_iota(jnp.int32, (8, PAIR), 1)
     pick = jnp.where((sub == 0) == (lane < HEAD_DIM), 1.0, 0.0).astype(BF16)
     dk[...] = jnp.zeros_like(dk)
     dv[...] = jnp.zeros_like(dv)
-    for g in range(group):
-        cols = slice(g * PAIR, (g + 1) * PAIR)
-        kt[cols, :length] = dot_t(ident, k_ref[:, cols]).astype(BF16)
-        kt[cols, length:] = dot_t(ident, pk_ref[:, cols]).astype(BF16)
-        prod = do_ref[:, cols].astype(F32) * mix_ref[:, cols].astype(F32)
-        high = prod.astype(BF16)
-        low = (prod - high.astype(F32)).astype(BF16)
-        delta[g] = dot_t(pick, high) + dot_t(pick, low)
-
-    def where_of(i):
-        g, qb = divmod(i, blocks)
+    kt[pair, :, :length] = dot_t(ident, k_ref[...]).astype(BF16)
+    kt[pair, :, length:] = dot_t(ident, pk_ref[...]).astype(BF16)
+    prod = do_ref[...].astype(F32) * mix_ref[...].astype(F32)
+    high = prod.astype(BF16)
+    rest = (prod - high.astype(F32)).astype(BF16)
+    delta[...] = dot_t(pick, high) + dot_t(pick, rest)
+
+    def where_of(qb):
         start = min(max(qb * QB - QB, 0), length - window)
-        return g, qb, slice(start, start + window), slice(qb * QB, (qb + 1) * QB), slice(g * PAIR, (g + 1) * PAIR)
-
-    def grad_probs(i):
-        g, qb, win, rows, cols = where_of(i)
-        vals = jnp.concatenate([v_ref[win, cols], pv_ref[:, cols]], axis=0)
-        gbuf[i % 2] = dot_t(vals, split_heads(do_ref[rows, cols]))
-
-    def grad_scores(i):
-        g, qb, win, rows, cols = where_of(i)
-        d = jnp.concatenate([delta[g, 0:1, rows], delta[g, 1:2, rows]], axis=1)
-        dsbuf[i % 2] = (p_ref[qb, g].astype(F32) * (gbuf[i % 2] - d)).astype(BF16)
-
-    def grads(i):
-        g, qb, win, rows, cols = where_of(i)
-        ds = dsbuf[i % 2]
-        dva = dot(p_ref[qb, g], split_heads(do_ref[rows, cols]))
-        dv[win, cols] += dva[:window]
-        dv[length:, cols] += dva[window:]
-        dka = dot(ds, split_heads(q_ref[rows, cols]))
-        dk[win, cols] += dka[:window]
-        dk[length:, cols] += dka[window:]
-        keys = jnp.concatenate([kt[cols, win], kt[cols, length:]], axis=1)
-        dqt[cols, rows] = own_blocks(dot(keys, ds) * HEAD_DIM ** -0.5).astype(BF16)
-
-    total = group * blocks
-    for i in range(total + 2):
-        if i < total:
+        return slice(start, start + window), slice(qb * QB, (qb + 1) * QB)
+
+    def grad_probs(qb):
+        win, rows = where_of(qb)
+        vals = jnp.concatenate([v_ref[win], pv_ref[...]], axis=0)
+        gbuf[qb % 2] = dot_t(vals, split_heads(do_ref[rows]))
+
+    def grad_scores(qb):
+        win, rows = where_of(qb)
+        d = jnp.concatenate([delta[0:1, rows], delta[1:2, rows]], axis=1)
+        ds_all[pair, qb] = (p_ref[qb, 0].astype(F32) * (gbuf[qb % 2] - d)).astype(BF16)
+
+    def grads(qb):
+        win, rows = where_of(qb)
+        dva = dot(p_ref[qb, 0], split_heads(do_ref[rows]))
+        dv[win] += dva[:window]
+        dv[length:] += dva[window:]
+        dka = dot(ds_all[pair, qb], split_heads(q_ref[rows]))
+        dk[win] += dka[:window]
+        dk[length:] += dka[window:]
+
+    for i in range(blocks + 2):
+        if i < blocks:
             grad_probs(i)
-        if 0 <= i - 1 < total:
+        if 0 <= i - 1 < blocks:
             grad_scores(i - 1)
-        if 0 <= i - 2 < total:
+        if 0 <= i - 2 < blocks:
             grads(i - 2)
-    gw = group * PAIR
-    big = eye(256)
-    for r in range(length // 256):
-        rr = slice(r * 256, (r + 1) * 256)
-        gj[step, rr, 0:gw] = dot_t(big, dqt[:, rr]).astype(BF16)
-    gj[step, :, gw:2 * gw] = dk[:length].astype(BF16)
-    gj[step, :, 2 * gw:] = dv[:length].astype(BF16)
-    gk_ref[...] = dk[length:]
-    gv_ref[...] = dv[length:]
-
-    @pl.when(step == pl.num_programs(0) - 1)
+    gj[pair, :, 0:PAIR] = dk[:length].astype(BF16)
+    gj[pair, :, PAIR:] = dv[:length].astype(BF16)
+    cols = pl.ds(pl.multiple_of(pair * PAIR, PAIR), PAIR)
+    each = 2 * pre // 8
+    for part, ref in enumerate((dk, dv)):
+        for i in range(4):
+            low[part * 4 + i, :, cols] = ref[length + i * each:length + (i + 1) * each].astype(BF16)
+
+    @pl.when(pair == pl.num_programs(0) - 1)
     def _():
-        steps = width // gw
+        total = Total(*counts, low, slots, parts, result, ((send0, recv0), (send1, recv1), (send2, recv2)))
+        total.first()
+
+        def query_grads(i, carry):
+            rows_of = pl.ds(pl.multiple_of(i * PAIR, PAIR), PAIR)
+            for qb in range(blocks):
+                win, rows = where_of(qb)
+                keys = jnp.concatenate([kt[i, :, win], kt[i, :, length:]], axis=1)
+                dqt[rows_of, rows] = own_blocks(dot(keys, ds_all[i, qb]) * HEAD_DIM ** -0.5).astype(BF16)
+            return carry
+
+        lax.fori_loop(0, pairs // 2, query_grads, 0)
+        total.second()
+        lax.fori_loop(pairs // 2, pairs, query_grads, 0)
+        total.third()
+        big = eye(256)
         for r in range(length // 256):
             rr = slice(r * 256, (r + 1) * 256)
-            acc = gone_ref[rr]
-            for part in range(3):
-                x = jnp.concatenate([gj[i, rr, part * gw:(part + 1) * gw] for i in range(steps)], axis=1)
-                acc = acc + dot_t(x, w_ref[:, part * width:(part + 1) * width])
+            acc = gone_ref[rr] + dot_t(dot_t(big, dqt[:, rr]).astype(BF16), w_ref[:, :width])
+            for part in range(2):
+                x = jnp.concatenate([gj[i, rr, part * PAIR:(part + 1) * PAIR] for i in range(pairs)], axis=1)
+                acc = acc + dot_t(x, w_ref[:, (part + 1) * width:(part + 2) * width])
             out_ref[rr] = acc.astype(BF16)
-
-
-def attend_backward(p, q, k, v, mix, do, pk, pv, wqkv, gone, group=2):
+        total.last()
+        for i in range(4):
+            gk_ref[i * each:(i + 1) * each] = result[i].astype(F32)
+            gv_ref[i * each:(i + 1) * each] = result[4 + i].astype(F32)
+
+
+def attend_backward(p, q, k, v, mix, do, pk, pv, wqkv, gone, counts):
     length, width = q.shape
     pre = pk.shape[0]
     blocks, pairs, depth, _ = p.shape
-    gw = group * PAIR
 
     def col(a):
-        return pl.BlockSpec((a.shape[0], gw), lambda i: (0, i))
-
-    out_spec, out_shape = kept((length, width), BF16)
+        return pl.BlockSpec((a.shape[0], PAIR), lambda i: (0, i))
+
+    outs = [kept((length, width), BF16)] + [kept((pre, width), F32)] * 2
+    count_q = counts[0] * counts[1] // 8
+    piece = (2 * pre // 8, width)
     return pl.pallas_call(
-        functools.partial(backward_kernel, group),
-        grid=(pairs // group,),
-        in_specs=[pl.BlockSpec((blocks, group, depth, 2 * QB), lambda i: (0, i, 0, 0))]
+        functools.partial(backward_kernel, counts),
+        grid=(pairs,),
+        in_specs=[pl.BlockSpec((blocks, 1, depth, 2 * QB), lambda i: (0, i, 0, 0))]
         + [col(a) for a in (q, k, v, mix, do, pk, pv)] + [whole(wqkv), whole(gone)],
-        out_specs=[out_spec, col(pk), col(pv)],
-        out_shape=[out_shape] + [jax.ShapeDtypeStruct((pre, width), F32)] * 2,
+        out_specs=[o[0] for o in outs],
+        out_shape=[o[1] for o in outs],
         scratch_shapes=[
-            pltpu.VMEM((gw, length + pre), BF16),
-            pltpu.VMEM((length + pre, gw), F32),
-            pltpu.VMEM((length + pre, gw), F32),
-            pltpu.VMEM((pairs // group, length, 3 * gw), BF16),
-            pltpu.VMEM((group, 8, length), F32),
+            pltpu.VMEM((pairs, PAIR, length + pre), BF16),
+            pltpu.VMEM((length + pre, PAIR), F32),
+            pltpu.VMEM((length + pre, PAIR), F32),
+            pltpu.VMEM((pairs, length, 2 * PAIR), BF16),
+            pltpu.VMEM((8, length), F32),
             pltpu.VMEM((2, depth, 2 * QB), F32),
-            pltpu.VMEM((2, depth, 2 * QB), BF16),
-            pltpu.VMEM((gw, length), BF16),
-        ],
-        compiler_params=pltpu.CompilerParams(vmem_limit_bytes=VMEM_LIMIT),
+            pltpu.VMEM((pairs, blocks, depth, 2 * QB), BF16),
+            pltpu.VMEM((width, length), BF16),
+            pltpu.VMEM((8,) + piece, BF16),
+            pltpu.VMEM((8,) + piece, BF16),
+            pltpu.VMEM((count_q,) + piece, BF16),
+            pltpu.VMEM((8,) + piece, BF16),
+        ] + [pltpu.SemaphoreType.DMA((n,)) for n in (8, 8, count_q, count_q, 8, 8)],
+        compiler_params=pltpu.CompilerParams(vmem_limit_bytes=VMEM_LIMIT, collective_id=1, has_side_effects=True),
         name="attend_backward",
     )(p, q, k, v, mix, do, pk, pv, wqkv, gone)
 
 
-def on_device(group, tokens, segment_ids, qkv_weight, prefix_keys, prefix_values, out_weight, out_bias, norm1_gain,
+def on_device(counts, tokens, segment_ids, qkv_weight, prefix_keys, prefix_values, out_weight, out_bias, norm1_gain,
               norm1_shift, up_weight, up_bias, down_weight, down_bias, norm2_gain, norm2_shift, out_grad):
     row = lambda a: a.reshape(1, -1)
     up_part = jnp.concatenate([up_weight, jnp.broadcast_to(row(up_bias), (BIAS_ROWS, up_bias.shape[0]))], axis=0)
     q, k, v, mix, probs, res, up_all, down_all = attend_forward(
-        tokens[0], qkv_weight, segment_ids, prefix_keys, prefix_values, out_weight, row(out_bias), up_part, down_weight, group)
+        tokens[0], qkv_weight, segment_ids, prefix_keys, prefix_values, out_weight, row(out_bias), up_part, down_weight, counts[1])
     out, grad_one, grad_mixed = feed_forward(
         res, out_grad[0], up_all, down_all, up_part, down_weight, out_weight, row(down_bias), row(norm1_gain), row(norm1_shift),
         row(norm2_gain), row(norm2_shift))
-    grad_tokens, gk, gv = attend_backward(
-        probs, q, k, v, mix, grad_mixed, prefix_keys, prefix_values, qkv_weight, grad_one)
-    total_k, total_v = lax.psum((gk, gv), ("dp", "mp"))
+    grad_tokens, total_k, total_v = attend_backward(
+        probs, q, k, v, mix, grad_mixed, prefix_keys, prefix_values, qkv_weight, grad_one, counts)
     return out[None], grad_tokens[None], total_k, total_v
 
 
 def solution(mesh):
     rows = P(("dp", "mp"), None, None)
     return jax.shard_map(
-        functools.partial(on_device, mesh.shape["mp"]),
+        functools.partial(on_device, (mesh.shape["dp"], mesh.shape["mp"])),
         mesh=mesh,
         in_specs=(rows, P(("dp", "mp"), None), P(), P(), P(), P(), P(), P(), P(), P(None, "mp"), P("mp"), P("mp", None),
                   P(), P(), P(), rows),

time: 320 us -> 190 us (0.59)
  waiting for transfers between devices: 127 us -> 0 us
  between operations: 14 us -> 0.67 us
  Pallas kernels: 173 us -> 182 us
    psum x1 -> x0, waiting for transfers between devices: 127 us -> none  [on_device(): total_k, total_v = lax.psum((gk, gv), ('dp', 'mp'))]
    pallas_call x1, Pallas kernels: 31.5 us -> 40.3 us  [attend_backward(): pl.pallas_call(functools.partial(backward_kernel, counts), grid=(pairs,),...]
  transfers between devices with their start and end apart: 1 -> 0, of which waited for: 1 -> 0; matrix products, arithmetic and copies ran while one was open for 0% -> 0% of each run, Pallas kernels for 0% -> 0%
where the time goes in v3:
time: 190 us
  Pallas kernels  182 us (96%)
  local copies, waits for them, and re-layouts  5.21 us (3%)
    pallas_call x1, Pallas kernels, attend_forward(): pl.pallas_call(functools.partial(forward_kernel, count_b), grid=(blocks,)...  85.2 us
    pallas_call x1, Pallas kernels, feed_forward(): pl.pallas_call(functools.partial(ffn_kernel, chunk), grid=(rows // tb,),...  56.2 us
    pallas_call x1, Pallas kernels, attend_backward(): pl.pallas_call(functools.partial(backward_kernel, counts), grid=(pairs,),...  40.3 us
    unnamed x7, local copies, waits for them, and re-layouts  4.55 us

profile of v3, /device:TPU:0, one launch (start us, length us, event | category | flops | bytes accessed | tf_op | source)
XLA Modules:
  0.0 189.5 jit_solution(797239514478453039)
XLA Ops:
  0.6 0.7 broadcast_in_dim.11
  1.3 1.9 pad_maximum_fusion.up_in.up_own
  3.2 85.2 %attend_forward.1 = (bf16[1024,1024]{1,0:T(8,128)(2,1)}, bf16[1024,1024]{1,0:T(8,128)(2,1)}, bf16[1024,1024]{1,0:T(8,128)(2,1)}, bf16[1024,1024]{1,0:T(8,128)(2,...) custom-call(bf16[1024,1024]{1,0:T(8,128)(2,1)} %bitcast.10, ...), custom_call_target="tpu_custom_call" | custom-call | tf_op jit(solution)/shard_map/attend_forward/pallas_call | solution.py:372
  88.4 56.2 %feed_forward.1 = (bf16[1024,1024]{1,0:T(8,128)(2,1)}, f32[1024,1024]{1,0:T(8,128)}, bf16[1024,1024]{1,0:T(8,128)(2,1)}) custom-call(f32[1024,1024]{1,0:T(8,128)} %get-tuple-element.18.res_ref, bf16[1024,1024]{1,0:T(8,128)(2,1)} %bitcast.12, bf16[16,1056,256]{2,1,0:T(8,128)(2,1)} %get-tuple-element.19.up_hbm, ...), custom_call_target="tpu_custom_call" | custom-call | tf_op jit(solution)/shard_map/feed_forward/pallas_call | solution.py:486
  144.6 40.3 %attend_backward.1 = (bf16[1024,1024]{1,0:T(8,128)(2,1)}, f32[64,1024]{1,0:T(8,128)}, f32[64,1024]{1,0:T(8,128)}) custom-call(bf16[8,8,448,256]{3,2,1,0:T(8,128)(2,1)} %get-tuple-element.22.p_ref, bf16[1024,1024]{1,0:T(8,128)(2,1)} %get-tuple-element.23.q_ref, bf16[1024,1024]{1,0:T(8,128)(2,1)} %get-tuple-element.24.k_ref, ...), custom_call_target="tpu_custom_call" | custom-call | tf_op jit(solution)/shard_map/attend_backward/pallas_call | solution.py:696
  185.0 0.0 copy-start.1
  185.0 0.0 copy-start
  185.0 3.1 %copy.23 = bf16[1,1024,1024]{2,1,0:T(8,128)(2,1)} copy(bf16[1,1024,1024]{2,1,0:T(8,128)(2,1)} %bitcast.11) | data formatting | bytes 4194304
  188.1 0.0 copy-done.1
  188.1 0.7 copy.24
  188.8 0.0 copy-done
  188.8 0.7 copy.25
Async XLA Ops:
  185.0 3.2 %copy-start.1 = (f32[64,1024]{1,0:T(8,128)S(1)}, f32[64,1024]{1,0:T(8,128)}, u32[]{:S(2)}) copy-start(f32[64,1024]{1,0:T(8,128)} %get-tuple-element.38) | copy-start | bytes 786436
  185.0 3.9 %copy-start = (f32[64,1024]{1,0:T(8,128)S(1)}, f32[64,1024]{1,0:T(8,128)}, u32[]{:S(2)}) copy-start(f32[64,1024]{1,0:T(8,128)} %get-tuple-element.39) | copy-start | bytes 786436

commit v4 on v3

--- a/solution.py
+++ b/solution.py
@@ -18,7 +18,20 @@
 BF16 = jnp.bfloat16
 VMEM_LIMIT = 62 * 1024 * 1024
 BIAS_ROWS = 32
-GATHER_SLOTS = ((0, 0, 0), (1, 1, 0), (2, 0, 1), (4, 1, 1), (5, 0, 2), (7, 1, 2), (8, 0, 3), (9, 1, 3), (9, 0, 4), (9, 1, 4))
+GATHER_SLOTS = (
+    (0, 0, 0, True), (0, 0, 0, False),
+    (2, 1, 0, True), (2, 1, 0, False),
+    (4, 0, 1, True),
+    (6, 1, 1, True), (6, 0, 1, False),
+    (7, 0, 2, True),
+    (8, 1, 1, False),
+    (9, 1, 2, True), (9, 0, 2, False),
+    (11, 0, 3, True), (11, 1, 2, False),
+    (12, 1, 3, True), (12, 0, 3, False),
+    (13, 1, 3, False),
+    (14, 0, 4, True), (14, 1, 4, True),
+    (15, 0, 4, False), (15, 1, 4, False),
+)
 
 
 def dot(a, b):
@@ -108,10 +121,9 @@
     return [
         [("x", s, 0, 0) for s in others] + [("z", side, 1, 0) for side in sides],
         [("z", side, 2, 0) for side in sides] + [("x", s, d, 0) for s in others for d in sides] + [("y", s, 0, 0) for s in others],
-        [("z", side, 3, 0) for side in sides] + [("x", s, 2, 0) for s in others] + [("z", side, 1, 1) for side in sides]
-        + [("y", s, d, 0) for s in others for d in sides],
-        [("y", 0, 3, 0)] + [("x", s, 3, 0) for s in others] + [("z", side, 2, 1) for side in sides],
-        [("y", s, 2, 0) for s in others] + [("x", s, 3, 1) for s in others],
+        [("z", side, 3, 0) for side in sides] + [("x", s, 2, 0) for s in others] + [("y", s, d, 0) for s in others for d in sides],
+        [("z", side, 1, 1) for side in sides] + [("y", 0, 3, 0)] + [("x", s, 3, 0) for s in others],
+        [("z", side, 2, 1) for side in sides] + [("y", s, 2, 0) for s in others] + [("x", s, 3, 1) for s in others],
     ]
 
 
@@ -242,33 +254,61 @@
 
         guarded(self.gets(key), body)
 
-    def level(self, t, n):
+    def level(self, t, n, along):
         for key in gather_events(self.count_b)[n]:
-            self.pass_on(t, key)
-        if n == 0:
+            if (key[0] == "z") == along:
+                self.pass_on(t, key)
+        if along and n < LINE - 1:
             for side in (1, -1):
-                self.start(t, "z", side, 1, 1)
-
-    def finish(self, t):
-        for key in self.keys:
-            if key[0] == "core":
+                sent = LINE - 1 - self.a if side == 1 else self.a
+                pl.when(sent == n)(lambda: self.start(t, "z", side, 1, 1))
+
+    def from_core(self, n, along):
+        keys = []
+        for kind, s, d, part in gather_events(self.count_b)[n]:
+            if (kind == "z") == along:
+                if kind == "z":
+                    key = ("core", 0, s if d == 1 else d, part)
+                else:
+                    key = ("core", s, d, 1 if kind == "y" else part)
+                if key not in keys:
+                    keys.append(key)
+        for t in range(2):
+            for key in keys:
                 guarded(self.gets(key), lambda: self.arrive(t, key))
+
+    def chip(self, o):
+        n = self.count_b - 1
+        end = self.a % 3 == 0
+        one, two, three = 1 + n, 1 + 2 * n, 4 + 2 * n
+        rank = jnp.where(o < one, 0, jnp.where(o <= two, 1, jnp.where(o == two + 1, jnp.where(end, 3, 2), jnp.where(
+            o == two + 2, jnp.where(end, 2, 3), jnp.where(o < three + n, 2, 3)))))
+        s = jnp.where(o < one, o, jnp.where(o < two, o - one + 1, jnp.where(o < three, 0, jnp.where(
+            o < three + n, o - three + 1, o - three - n + 1))))
+        a = jnp.where(rank == 0, self.a, jnp.where(rank == 1, 1 + self.a % 2, jnp.where(
+            rank == 2, (2 + 3 * self.a) % 5, 3 - 3 * (self.a // 2))))
+        return a * self.count_b + (self.b + s) % self.count_b
 
     def close(self, t):
         for key in self.keys:
             guarded(self.sends(key), lambda: self.copy(t, key, False).wait_send())
 
 
-def forward_kernel(count_b, tok_ref, wqkv_ref, seg_ref, pk_ref, pv_ref, wo_ref, bo_ref, up_in, down_in,
-                   q_out, k_out, v_out, mix_out, p_out, res_out, up_all, down_all,
-                   vt, pvt, segc, bias, sbuf, mixt, send, recv):
+def forward_kernel(count_b, tok_ref, wqkv_hbm, seg_ref, pk_ref, pv_ref, wo_ref, bo_ref, g1_ref, s1_ref, db_ref, up_in, down_in,
+                   q_hbm, k_hbm, v_hbm, mix_hbm, p_out, res_hbm, two_hbm, up_all, down_all, slope_out,
+                   q_out, k_out, v_out, mix_out, res_out, two, wqkv_ref, vt, pvt, segc, bias, sbuf, mixt, low, up_v, down_v, pre, hid, slope, send, recv, wsem, qsem, osem, xsem):
     qb = pl.program_id(0)
+
+    def copy_out(n):
+        src = (q_out, k_out, v_out, mix_out, res_out, two)[n]
+        return pltpu.make_async_copy(src, (q_hbm, k_hbm, v_hbm, mix_hbm, res_hbm, two_hbm)[n], xsem.at[n])
+
     gather = Gather(count_b, (up_in, down_in), (up_all, down_all), (send, recv))
 
     def pass_on(now):
-        for slot, t, n in GATHER_SLOTS:
+        for slot, t, n, along in GATHER_SLOTS:
             if slot == now:
-                gather.level(t, n)
+                gather.level(t, n, along)
 
     length, width = tok_ref.shape
     window = bias.shape[0]
@@ -276,23 +316,30 @@
 
     @pl.when(qb == 0)
     def _():
+        def weights(part):
+            cols = pl.ds(part * width, width)
+            return pltpu.make_async_copy(wqkv_hbm.at[:, cols], wqkv_ref.at[:, cols], qsem.at[part])
+
+        for part in range(3):
+            weights(part).start()
         gather.greet()
         gather.open(0)
         gather.open(1)
         tile = 256
         for part, ref in enumerate((q_out, k_out, v_out)):
+            weights(part).wait()
             for j in range(width // tile):
                 x = dot(tok_ref[...], wqkv_ref[:, part * width + j * tile:part * width + (j + 1) * tile]).astype(BF16)
                 if part == 0:
                     x = x * jnp.asarray(HEAD_DIM ** -0.5, BF16)
                 ref[:, j * tile:(j + 1) * tile] = x
-                if part == 2 and j == 2:
-                    pass_on(0)
+            copy_out(part).start()
         big = eye(256)
         for j in range(width // 256):
             cols = slice(j * 256, (j + 1) * 256)
             vt[cols, :] = dot_t(big, v_out[:, cols]).astype(BF16)
             pvt[cols, :] = dot_t(big, pv_ref[:, cols]).astype(BF16)
+        pass_on(0)
         ident = eye(QB)
         seg = jnp.broadcast_to(seg_ref[...].astype(F32), (QB, length)).astype(BF16)
         for j in range(length // QB):
@@ -346,122 +393,216 @@
         for r in range(length // 256):
             rr = slice(r * 256, (r + 1) * 256)
             mix_out[rr] = dot_t(big, mixt[:, rr]).astype(BF16)
+        copy_out(3).start()
         for r in range(length // 256):
             rr = slice(r * 256, (r + 1) * 256)
-            res_out[rr] = tok_ref[rr].astype(F32) + dot(mix_out[rr], wo_ref[...]) + bo_ref[...]
+            res = tok_ref[rr].astype(F32) + dot(mix_out[rr], wo_ref[...]) + bo_ref[...]
+            res_out[rr] = res
+            first = normalize(res)[0] * g1_ref[...] + s1_ref[...]
+            low[rr] = first.astype(BF16)
+            two[rr] = first + db_ref[...]
+        copy_out(4).start()
         pass_on(9)
+
+        chips = LINE * count_b
+        ffl = down_in.shape[0]
+        per = length // 256
+
+        def loads(o):
+            chip = gather.chip(o)
+            out = []
+            for c in range(2):
+                core = gather.core if c else 1 - gather.core
+                cols = pl.ds(pl.multiple_of(core * ffl, 128), ffl)
+                own = isinstance(o, int) and o == 0 and c == 1
+                for t, to in ((0, up_v.at[o % 3, :, cols]), (1, down_v.at[o % 3, cols])):
+                    src = (up_in, down_in)[t] if own else (up_all, down_all)[t].at[2 * chip + core]
+                    out.append(pltpu.make_async_copy(src, to, wsem.at[o % 3, t, c]))
+            return out
+
+        def load(o):
+            for copy in loads(o):
+                copy.start()
+
+        def loaded(o):
+            for copy in loads(o):
+                copy.wait()
+
+        def rows_of(b):
+            return slice(b * 256, (b + 1) * 256)
+
+        def up(o, b):
+            pre[b % 2] = dot(low[rows_of(b)], up_v[o % 3, :width, :])
+
+        def act(o, b):
+            u = pre[b % 2] + up_v[o % 3, width:width + 1, :].astype(F32)
+            half = 0.5 * lax.erf(u * ROOT_HALF) + 0.5
+            hid[b % 2] = (u * half).astype(BF16)
+            slope[o, rows_of(b)] = (half + u * (jnp.exp(-0.5 * u * u) * INV_ROOT_TWOPI)).astype(BF16)
+
+        def down(o, b):
+            two[rows_of(b)] += dot(hid[b % 2], down_v[o % 3])
+
+        def earlier(o, b, n):
+            return (o, b - n) if b >= n else (o - 1, b - n + per)
+
+        def chip_steps(o, ahead):
+            loaded(o)
+            for b in range(per):
+                if b == 2:
+                    ahead()
+                up(o, b)
+                if b >= 1 or not (isinstance(o, int) and o == 0):
+                    act(*earlier(o, b, 1))
+                if b >= 2 or not (isinstance(o, int) and o == 0):
+                    down(*earlier(o, b, 2))
+
+        def keep(o):
+            return pltpu.make_async_copy(slope.at[o], slope_out.at[gather.chip(o)], osem.at[o])
+
+        def more():
+            pass_on(10)
+            for n in range(2):
+                for along in (True, False):
+                    gather.from_core(n, along)
+
         for t in range(2):
-            gather.finish(t)
+            gather.arrive(t, ("core", 0, 0, None))
+        load(0)
+
+        def first_ahead():
+            more()
+            load(1)
+
+        chip_steps(0, first_ahead)
+        others = count_b - 1
+        needs = ((others, 11, 2, (True, False)), (2 * others, 12, 3, (True,)), (2 * others + 1, 13, 3, (False,)),
+                 (2 * others + 2, 14, 4, (True,)), (2 * others + 3, 15, 4, (False,)))
+
+        def chip_step(o, carry):
+            def ahead():
+                for at, slot, n, kinds in needs:
+
+                    @pl.when(o == at)
+                    def _():
+                        pass_on(slot)
+                        for along in kinds:
+                            gather.from_core(n, along)
+
+                @pl.when(o < chips - 1)
+                def _():
+                    load(o + 1)
+
+            chip_steps(o, ahead)
+            return carry
+
+        lax.fori_loop(1, chips, chip_step, 0)
+        act(chips - 1, per - 1)
+        down(chips - 1, per - 2)
+        down(chips - 1, per - 1)
+        copy_out(5).start()
+        for o in range(chips):
+            keep(o).start()
         for t in range(2):
             gather.close(t)
-
-
-def attend_forward(tok, wqkv, seg, pk, pv, wo, bo, up, down, group):
+        for o in range(chips):
+            keep(o).wait()
+        for n in range(6):
+            copy_out(n).wait()
+
+
+def attend_forward(tok, wqkv, seg, pk, pv, wo, bo, g1, s1, db, up, down, group):
     length, width = tok.shape
     pre = pk.shape[0]
     window = 3 * QB
     pairs, blocks = width // PAIR, length // QB
-    outs = [kept((length, width), BF16)] * 4 + [
+    hbm = pl.BlockSpec(memory_space=pl.ANY)
+    square, wide = jax.ShapeDtypeStruct((length, width), BF16), jax.ShapeDtypeStruct((length, width), F32)
+    outs = [(hbm, square)] * 4 + [
         (pl.BlockSpec((1, pairs, window + pre, 2 * QB), lambda i: (i, 0, 0, 0)),
          jax.ShapeDtypeStruct((blocks, pairs, window + pre, 2 * QB), BF16)),
-        kept((length, width), F32)]
-    hbm = pl.BlockSpec(memory_space=pl.ANY)
+        (hbm, wide), (hbm, wide)]
     outs += [(hbm, jax.ShapeDtypeStruct((group,) + a.shape, BF16)) for a in (up, down)]
+    chips, part = group // 2, 2 * down.shape[0]
+    outs += [(hbm, jax.ShapeDtypeStruct((chips, length, part), BF16))]
     count_b = group // (2 * LINE)
     pieces = len(gather_keys(count_b))
     return pl.pallas_call(
         functools.partial(forward_kernel, count_b),
         grid=(blocks,),
-        in_specs=[whole(a) for a in (tok, wqkv, seg, pk, pv, wo, bo)] + [hbm, hbm],
+        in_specs=[whole(tok), hbm] + [whole(a) for a in (seg, pk, pv, wo, bo, g1, s1, db)] + [hbm, hbm],
         out_specs=[o[0] for o in outs],
         out_shape=[o[1] for o in outs],
-        scratch_shapes=[
+        scratch_shapes=[pltpu.VMEM((length, width), t) for t in (BF16, BF16, BF16, BF16, F32, F32)] + [
+            pltpu.VMEM(wqkv.shape, BF16),
             pltpu.VMEM((width, length), BF16),
             pltpu.VMEM((width, pre), BF16),
             pltpu.VMEM((length, QB), F32),
             pltpu.VMEM((window, QB), F32),
             pltpu.VMEM((2, window + pre, 2 * QB), F32),
             pltpu.VMEM((width, length), BF16),
+            pltpu.VMEM((length, width), BF16),
+            pltpu.VMEM((3, up.shape[0], part), BF16),
+            pltpu.VMEM((3, part, width), BF16),
+            pltpu.VMEM((2, 256, part), F32),
+            pltpu.VMEM((2, 256, part), BF16),
+            pltpu.VMEM((chips, length, part), BF16),
             pltpu.SemaphoreType.DMA((2, pieces)),
             pltpu.SemaphoreType.DMA((2, pieces)),
+            pltpu.SemaphoreType.DMA((3, 2, 2)),
+            pltpu.SemaphoreType.DMA((3,)),
+            pltpu.SemaphoreType.DMA((chips,)),
+            pltpu.SemaphoreType.DMA((6,)),
         ],
         compiler_params=pltpu.CompilerParams(vmem_limit_bytes=VMEM_LIMIT, collective_id=0, has_side_effects=True),
         name="attend_forward",
-    )(tok, wqkv, seg, pk, pv, wo, bo, up, down)
-
-
-def ffn_kernel(chunk, res_ref, dy_ref, up_hbm, down_hbm, up_own, down_own, wo_ref, db_ref, g1_ref, s1_ref, g2_ref, s2_ref,
-               out_ref, gone_ref, gmix_ref, up, down, ub, pre, hid, slope, low, acc, hat_s, sems):
+    )(tok, wqkv, seg, pk, pv, wo, bo, g1, s1, db, up, down)
+
+
+def ffn_kernel(res_ref, two_ref, dy_ref, slope_ref, up_hbm, down_hbm, up_own, down_own, wo_ref, g1_ref, g2_ref, s2_ref,
+               out_ref, gone_ref, gmix_ref, up, down, hid, low, acc, sems):
     step = pl.program_id(0)
-    count = up.shape[1] // chunk
     width = up.shape[0]
-    parts, _, part = up_hbm.shape
-
+    parts, part, _ = down_hbm.shape
+    count, _, chunk = slope_ref.shape
     me = lax.axis_index("mp")
 
-    def fetch(d, t):
+    def fetch(d, t, own):
         cols = pl.ds(d * part, part)
-        up_src, down_src = (up_own, down_own) if d == 0 else (up_hbm.at[(me + d) % parts], down_hbm.at[(me + d) % parts])
-        src = (up_src.at[pl.ds(0, width)], up_src.at[pl.ds(width, BIAS_ROWS)], down_src)[t]
-        dst = (up.at[:, cols], ub.at[:, cols], down.at[cols])[t]
+        up_src, down_src = (up_own, down_own) if own else (up_hbm.at[d], down_hbm.at[d])
+        src, dst = ((up_src.at[pl.ds(0, width)], up.at[:, cols]), (down_src, down.at[cols]))[t]
         return pltpu.make_async_copy(src, dst, sems.at[t, d])
 
     @pl.when(step == 0)
     def _():
-        for t in range(3):
+        for t in (1, 0):
             for d in range(parts):
-                fetch(d, t).start()
-
-    hat, inv1 = normalize(res_ref[...])
-    hat_s[...] = hat
-    low[...] = (hat * g1_ref[...] + s1_ref[...]).astype(BF16)
-
-    @pl.when(step == 0)
-    def _():
-        for t in range(2):
-            for d in range(parts):
-                fetch(d, t).wait()
-
-    def cols_of(j):
-        return slice(j * chunk, (j + 1) * chunk)
-
-    def rows_up(j):
-        pre[j % 2] = dot(low[...], up[:, cols_of(j)])
-
-    def act(j):
-        u = pre[j % 2] + ub[0:1, cols_of(j)].astype(F32)
-        half = 0.5 * lax.erf(u * ROOT_HALF) + 0.5
-        hid[j % 2] = (u * half).astype(BF16)
-        slope[:, cols_of(j)] = (half + u * (jnp.exp(-0.5 * u * u) * INV_ROOT_TWOPI)).astype(BF16)
-
-    def rows_down(j):
-        acc[...] += dot(hid[j % 2], down[cols_of(j)])
-
-    acc[...] = jnp.zeros_like(acc)
-    for j in range(count + 2):
-        if j == 2:
-
-            @pl.when(step == 0)
-            def _():
-                for d in range(parts):
-                    fetch(d, 2).wait()
-
-        if j < count:
-            rows_up(j)
-        if 0 <= j - 2 < count:
-            rows_down(j - 2)
-        if 0 <= j - 1 < count:
-            act(j - 1)
-
-    hat2, inv2 = normalize(hat_s[...] * g1_ref[...] + s1_ref[...] + acc[...] + db_ref[...])
+
+                @pl.when(me == d)
+                def _():
+                    fetch(d, t, True).start()
+
+                @pl.when(me != d)
+                def _():
+                    fetch(d, t, False).start()
+
+    hat2, inv2 = normalize(two_ref[...])
     out_ref[...] = (hat2 * g2_ref[...] + s2_ref[...]).astype(BF16)
     grad_two = norm_back(dy_ref[...].astype(F32), hat2, inv2, g2_ref[...])
     acc[...] = grad_two
     low[...] = grad_two.astype(BF16)
 
+    @pl.when(step == 0)
+    def _():
+        for d in range(parts):
+            fetch(d, 1, False).wait()
+
+    def cols_of(j):
+        return slice(j * chunk, (j + 1) * chunk)
+
     def back_down(j):
         gh = dot_t(low[...], down[cols_of(j)])
-        hid[j % 2] = (gh * slope[:, cols_of(j)].astype(F32)).astype(BF16)
+        hid[j % 2] = (gh * slope_ref[j].astype(F32)).astype(BF16)
 
     def back_up(j):
         acc[...] += dot_t(hid[j % 2], up[:, cols_of(j)])
@@ -469,41 +610,47 @@
     for j in range(count + 1):
         if j < count:
             back_down(j)
+        if j == 1:
+
+            @pl.when(step == 0)
+            def _():
+                for d in range(parts):
+                    fetch(d, 0, False).wait()
+
         if j >= 1:
             back_up(j - 1)
 
-    grad_one = norm_back(acc[...], hat_s[...], inv1, g1_ref[...])
+    hat, inv1 = normalize(res_ref[...])
+    grad_one = norm_back(acc[...], hat, inv1, g1_ref[...])
     gone_ref[...] = grad_one
     gmix_ref[...] = dot_t(grad_one.astype(BF16), wo_ref[...]).astype(BF16)
 
 
-def feed_forward(res, dy, up, down, up_own, down_own, wo, db, g1, s1, g2, s2, tb=256, chunk=512):
+def feed_forward_backward(res, two, dy, slope, up, down, up_own, down_own, wo, g1, g2, s2, tb=256):
     rows, width = res.shape
     parts, ffl, _ = down.shape
     ff = parts * ffl
+    chips, _, part = slope.shape
     block = pl.BlockSpec((tb, width), lambda i: (i, 0))
     hbm = pl.BlockSpec(memory_space=pl.ANY)
     return pl.pallas_call(
-        functools.partial(ffn_kernel, chunk),
+        ffn_kernel,
         grid=(rows // tb,),
-        in_specs=[block, block] + [hbm] * 4 + [whole(a) for a in (wo, db, g1, s1, g2, s2)],
+        in_specs=[block] * 3 + [pl.BlockSpec((chips, tb, part), lambda i: (0, i, 0))] + [hbm] * 4
+        + [whole(a) for a in (wo, g1, g2, s2)],
         out_specs=[block] * 3,
         out_shape=[jax.ShapeDtypeStruct((rows, width), t) for t in (BF16, F32, BF16)],
         scratch_shapes=[
             pltpu.VMEM((width, ff), BF16),
             pltpu.VMEM((ff, width), BF16),
-            pltpu.VMEM((BIAS_ROWS, ff), BF16),
-            pltpu.VMEM((2, tb, chunk), F32),
-            pltpu.VMEM((2, tb, chunk), BF16),
-            pltpu.VMEM((tb, ff), BF16),
+            pltpu.VMEM((2, tb, part), BF16),
             pltpu.VMEM((tb, width), BF16),
             pltpu.VMEM((tb, width), F32),
-            pltpu.VMEM((tb, width), F32),
-            pltpu.SemaphoreType.DMA((3, parts)),
+            pltpu.SemaphoreType.DMA((2, parts)),
         ],
         compiler_params=pltpu.CompilerParams(vmem_limit_bytes=VMEM_LIMIT),
-        name="feed_forward",
-    )(res, dy, up, down, up_own, down_own, wo, db, g1, s1, g2, s2)
+        name="feed_forward_backward",
+    )(res, two, dy, slope, up, down, up_own, down_own, wo, g1, g2, s2)
 
 
 class Total:
@@ -590,10 +737,17 @@
                 self.copy(phase, j).wait_send()
 
 
-def backward_kernel(counts, p_ref, q_ref, k_ref, v_ref, mix_ref, do_ref, pk_ref, pv_ref, w_ref, gone_ref,
-                    out_ref, gk_ref, gv_ref, kt, dk, dv, gj, delta, gbuf, ds_all, dqt, low, slots, parts, result,
-                    send0, recv0, send1, recv1, send2, recv2):
+def backward_kernel(counts, p_ref, q_ref, k_ref, v_ref, mix_ref, do_ref, pk_ref, pv_ref, w_hbm, gone_hbm,
+                    out_ref, gk_ref, gv_ref, w_ref, gone_ref, kt, dk, dv, gj, delta, gbuf, ds_all, dqt, low, slots, parts, result,
+                    send0, recv0, send1, recv1, send2, recv2, late):
     pair = pl.program_id(0)
+    loads = [pltpu.make_async_copy(w_hbm, w_ref, late.at[0]), pltpu.make_async_copy(gone_hbm, gone_ref, late.at[1])]
+
+    @pl.when(pair == 0)
+    def _():
+        for copy in loads:
+            copy.start()
+
     length = q_ref.shape[0]
     pre = pk_ref.shape[0]
     pairs, width = ds_all.shape[0], out_ref.shape[1]
@@ -668,6 +822,8 @@
         total.second()
         lax.fori_loop(pairs // 2, pairs, query_grads, 0)
         total.third()
+        for copy in loads:
+            copy.wait()
         big = eye(256)
         for r in range(length // 256):
             rr = slice(r * 256, (r + 1) * 256)
@@ -697,10 +853,12 @@
         functools.partial(backward_kernel, counts),
         grid=(pairs,),
         in_specs=[pl.BlockSpec((blocks, 1, depth, 2 * QB), lambda i: (0, i, 0, 0))]
-        + [col(a) for a in (q, k, v, mix, do, pk, pv)] + [whole(wqkv), whole(gone)],
+        + [col(a) for a in (q, k, v, mix, do, pk, pv)] + [pl.BlockSpec(memory_space=pl.ANY)] * 2,
         out_specs=[o[0] for o in outs],
         out_shape=[o[1] for o in outs],
         scratch_shapes=[
+            pltpu.VMEM(wqkv.shape, BF16),
+            pltpu.VMEM((length, width), F32),
             pltpu.VMEM((pairs, PAIR, length + pre), BF16),
             pltpu.VMEM((length + pre, PAIR), F32),
             pltpu.VMEM((length + pre, PAIR), F32),
@@ -713,7 +871,7 @@
             pltpu.VMEM((8,) + piece, BF16),
             pltpu.VMEM((count_q,) + piece, BF16),
             pltpu.VMEM((8,) + piece, BF16),
-        ] + [pltpu.SemaphoreType.DMA((n,)) for n in (8, 8, count_q, count_q, 8, 8)],
+        ] + [pltpu.SemaphoreType.DMA((n,)) for n in (8, 8, count_q, count_q, 8, 8, 2)],
         compiler_params=pltpu.CompilerParams(vmem_limit_bytes=VMEM_LIMIT, collective_id=1, has_side_effects=True),
         name="attend_backward",
     )(p, q, k, v, mix, do, pk, pv, wqkv, gone)
@@ -723,11 +881,12 @@
               norm1_shift, up_weight, up_bias, down_weight, down_bias, norm2_gain, norm2_shift, out_grad):
     row = lambda a: a.reshape(1, -1)
     up_part = jnp.concatenate([up_weight, jnp.broadcast_to(row(up_bias), (BIAS_ROWS, up_bias.shape[0]))], axis=0)
-    q, k, v, mix, probs, res, up_all, down_all = attend_forward(
-        tokens[0], qkv_weight, segment_ids, prefix_keys, prefix_values, out_weight, row(out_bias), up_part, down_weight, counts[1])
-    out, grad_one, grad_mixed = feed_forward(
-        res, out_grad[0], up_all, down_all, up_part, down_weight, out_weight, row(down_bias), row(norm1_gain), row(norm1_shift),
-        row(norm2_gain), row(norm2_shift))
+    q, k, v, mix, probs, res, two, up_all, down_all, slope = attend_forward(
+        tokens[0], qkv_weight, segment_ids, prefix_keys, prefix_values, out_weight, row(out_bias), row(norm1_gain),
+        row(norm1_shift), row(down_bias), up_part, down_weight, counts[1])
+    out, grad_one, grad_mixed = feed_forward_backward(
+        res, two, out_grad[0], slope, up_all, down_all, up_part, down_weight, out_weight, row(norm1_gain), row(norm2_gain),
+        row(norm2_shift))
     grad_tokens, total_k, total_v = attend_backward(
         probs, q, k, v, mix, grad_mixed, prefix_keys, prefix_values, qkv_weight, grad_one, counts)
     return out[None], grad_tokens[None], total_k, total_v

time: 190 us -> 176 us (0.926)
  Pallas kernels: 182 us -> 168 us
    pallas_call x1, Pallas kernels: 56.2 us -> 34.6 us  [feed_forward_backward(): pl.pallas_call(ffn_kernel, grid=(rows // tb,), in_specs=[block] * 3 + [pl...]
    pallas_call x1, Pallas kernels: 85.2 us -> 92.4 us  [attend_forward(): pl.pallas_call(functools.partial(forward_kernel, count_b), grid=(blocks,)...]
where the time goes in v4:
time: 176 us
  Pallas kernels  168 us (95%)
  local copies, waits for them, and re-layouts  5.21 us (3%)
  other arithmetic  1.88 us (1%)
    pallas_call x1, Pallas kernels, attend_forward(): pl.pallas_call(functools.partial(forward_kernel, count_b), grid=(blocks,)...  92.4 us
    pallas_call x1, Pallas kernels, attend_backward(): pl.pallas_call(functools.partial(backward_kernel, counts), grid=(pairs,),...  40.9 us
    pallas_call x1, Pallas kernels, feed_forward_backward(): pl.pallas_call(ffn_kernel, grid=(rows // tb,), in_specs=[block] * 3 + [pl...  34.6 us
    unnamed x7, local copies, waits for them, and re-layouts  4.55 us

profile of v4, /device:TPU:0, one launch (start us, length us, event | category | flops | bytes accessed | tf_op | source)
XLA Modules:
  0.0 175.7 jit_solution(16136687195971443190)
XLA Ops:
  0.6 0.7 broadcast_in_dim.11
  1.3 1.9 %pad_maximum_fusion.up_in.up_own = bf16[1056,256]{1,0:T(8,128)(2,1)} fusion(bf16[32,256]{1,0:T(8,128)(2,1)S(1)} %broadcast_in_dim.11, bf16[1024,256]{1,0:T(8,128)(2,1)} %param.25), kind=kLoop, calls=%fused_computation | loop fusion | flops 1081344 | bytes 1081344 | tf_op jit(solution)/shard_map/concatenate | solution.py:883
  3.2 92.4 %attend_forward.1 = (bf16[1024,1024]{1,0:T(8,128)(2,1)}, bf16[1024,1024]{1,0:T(8,128)(2,1)}, bf16[1024,1024]{1,0:T(8,128)(2,1)}, bf16[1024,1024]{1,0:T(8,128)(2,...) custom-call(bf16[1024,1024]{1,0:T(8,128)(2,1)} %bitcast.11, ...), custom_call_target="tpu_custom_call" | custom-call | tf_op jit(solution)/shard_map/attend_forward/pallas_call | solution.py:530
  95.6 34.6 %feed_forward_backward.1 = (bf16[1024,1024]{1,0:T(8,128)(2,1)}, f32[1024,1024]{1,0:T(8,128)}, bf16[1024,1024]{1,0:T(8,128)(2,1)}) custom-call(f32[1024,1024]{1,0:T(8,128)} %get-tuple-element.20.res_ref, f32[1024,1024]{1,0:T(8,128)} %get-tuple-element.21.two_ref, bf16[1024,1024]{1,0:T(8,128)(2,1)} %bitcast.12, ...), custom_call_target="tpu_custom_call" | custom-call | tf_op jit(solution)/shard_map/feed_forward_backward/pallas_call | solution.py:636
  130.2 40.9 %attend_backward.1 = (bf16[1024,1024]{1,0:T(8,128)(2,1)}, f32[64,1024]{1,0:T(8,128)}, f32[64,1024]{1,0:T(8,128)}) custom-call(bf16[8,8,448,256]{3,2,1,0:T(8,128)(2,1)} %get-tuple-element.26.p_ref, bf16[1024,1024]{1,0:T(8,128)(2,1)} %get-tuple-element.27.q_ref, bf16[1024,1024]{1,0:T(8,128)(2,1)} %get-tuple-element.28.k_ref, ...), custom_call_target="tpu_custom_call" | custom-call | tf_op jit(solution)/shard_map/attend_backward/pallas_call | solution.py:852
  171.1 0.0 copy-start.1
  171.1 0.0 copy-start
  171.1 3.1 %copy.23 = bf16[1,1024,1024]{2,1,0:T(8,128)(2,1)} copy(bf16[1,1024,1024]{2,1,0:T(8,128)(2,1)} %bitcast.10) | data formatting | bytes 4194304
  174.2 0.0 copy-done.1
  174.3 0.7 copy.24
  175.0 0.0 copy-done
  175.0 0.7 copy.25
Async XLA Ops:
  171.1 3.2 %copy-start.1 = (f32[64,1024]{1,0:T(8,128)S(1)}, f32[64,1024]{1,0:T(8,128)}, u32[]{:S(2)}) copy-start(f32[64,1024]{1,0:T(8,128)} %get-tuple-element.42) | copy-start | bytes 786436
  171.1 3.9 %copy-start = (f32[64,1024]{1,0:T(8,128)S(1)}, f32[64,1024]{1,0:T(8,128)}, u32[]{:S(2)}) copy-start(f32[64,1024]{1,0:T(8,128)} %get-tuple-element.43) | copy-start | bytes 786436

commit v5 on v4

--- a/solution.py
+++ b/solution.py
@@ -17,9 +17,11 @@
 F32 = jnp.float32
 BF16 = jnp.bfloat16
 VMEM_LIMIT = 62 * 1024 * 1024
+BACKWARD_LIMIT = 56 * 1024 * 1024
 BIAS_ROWS = 32
+QKV_SLOT = (1, 1)
 GATHER_SLOTS = (
-    (0, 0, 0, True), (0, 0, 0, False),
+    (16, 0, 0, True), (16, 0, 0, False),
     (2, 1, 0, True), (2, 1, 0, False),
     (4, 0, 1, True),
     (6, 1, 1, True), (6, 0, 1, False),
@@ -294,9 +296,9 @@
             guarded(self.sends(key), lambda: self.copy(t, key, False).wait_send())
 
 
-def forward_kernel(count_b, tok_ref, wqkv_hbm, seg_ref, pk_ref, pv_ref, wo_ref, bo_ref, g1_ref, s1_ref, db_ref, up_in, down_in,
+def forward_kernel(count_b, tok_hbm, wqkv_hbm, wo_hbm, up_hbm, down_in, seg_ref, pk_ref, pv_ref, bo_ref, g1_ref, s1_ref, db_ref, ub_ref,
                    q_hbm, k_hbm, v_hbm, mix_hbm, p_out, res_hbm, two_hbm, up_all, down_all, slope_out,
-                   q_out, k_out, v_out, mix_out, res_out, two, wqkv_ref, vt, pvt, segc, bias, sbuf, mixt, low, up_v, down_v, pre, hid, slope, send, recv, wsem, qsem, osem, xsem):
+                   q_out, k_out, v_out, mix_out, res_out, two, tok_ref, wo_ref, up_in, wqkv_ref, vt, pvt, segc, bias, sbuf, mixt, low, up_v, down_v, pre, hid, slope, send, recv, wsem, qsem, osem, xsem):
     qb = pl.program_id(0)
 
     def copy_out(n):
@@ -320,12 +322,20 @@
             cols = pl.ds(part * width, width)
             return pltpu.make_async_copy(wqkv_hbm.at[:, cols], wqkv_ref.at[:, cols], qsem.at[part])
 
+        whole_in = [pltpu.make_async_copy(src, dst, qsem.at[3 + n]) for n, (src, dst) in enumerate((
+            (up_hbm, up_in.at[pl.ds(0, width)]), (tok_hbm, tok_ref), (wo_hbm, wo_ref)))]
+        whole_in[0].start()
+        whole_in[1].start()
         for part in range(3):
             weights(part).start()
+        whole_in[2].start()
+        up_in[width:] = jnp.broadcast_to(ub_ref[...].astype(F32), (BIAS_ROWS, ub_ref.shape[1])).astype(BF16)
         gather.greet()
+        whole_in[0].wait()
         gather.open(0)
         gather.open(1)
         tile = 256
+        whole_in[1].wait()
         for part, ref in enumerate((q_out, k_out, v_out)):
             weights(part).wait()
             for j in range(width // tile):
@@ -333,7 +343,10 @@
                 if part == 0:
                     x = x * jnp.asarray(HEAD_DIM ** -0.5, BF16)
                 ref[:, j * tile:(j + 1) * tile] = x
+                if (part, j) == QKV_SLOT:
+                    pass_on(16)
             copy_out(part).start()
+        whole_in[2].wait()
         big = eye(256)
         for j in range(width // 256):
             cols = slice(j * 256, (j + 1) * 256)
@@ -448,9 +461,8 @@
 
         def chip_steps(o, ahead):
             loaded(o)
+            ahead()
             for b in range(per):
-                if b == 2:
-                    ahead()
                 up(o, b)
                 if b >= 1 or not (isinstance(o, int) and o == 0):
                     act(*earlier(o, b, 1))
@@ -494,6 +506,7 @@
                     load(o + 1)
 
             chip_steps(o, ahead)
+            keep(o - 1).start()
             return carry
 
         lax.fori_loop(1, chips, chip_step, 0)
@@ -501,8 +514,7 @@
         down(chips - 1, per - 2)
         down(chips - 1, per - 1)
         copy_out(5).start()
-        for o in range(chips):
-            keep(o).start()
+        keep(chips - 1).start()
         for t in range(2):
             gather.close(t)
         for o in range(chips):
@@ -511,7 +523,7 @@
             copy_out(n).wait()
 
 
-def attend_forward(tok, wqkv, seg, pk, pv, wo, bo, g1, s1, db, up, down, group):
+def attend_forward(tok, wqkv, wo, up, down, seg, pk, pv, bo, g1, s1, db, ub, group):
     length, width = tok.shape
     pre = pk.shape[0]
     window = 3 * QB
@@ -522,7 +534,8 @@
         (pl.BlockSpec((1, pairs, window + pre, 2 * QB), lambda i: (i, 0, 0, 0)),
          jax.ShapeDtypeStruct((blocks, pairs, window + pre, 2 * QB), BF16)),
         (hbm, wide), (hbm, wide)]
-    outs += [(hbm, jax.ShapeDtypeStruct((group,) + a.shape, BF16)) for a in (up, down)]
+    up_shape = (width + BIAS_ROWS, up.shape[1])
+    outs += [(hbm, jax.ShapeDtypeStruct((group,) + shape, BF16)) for shape in (up_shape, down.shape)]
     chips, part = group // 2, 2 * down.shape[0]
     outs += [(hbm, jax.ShapeDtypeStruct((chips, length, part), BF16))]
     count_b = group // (2 * LINE)
@@ -530,10 +543,12 @@
     return pl.pallas_call(
         functools.partial(forward_kernel, count_b),
         grid=(blocks,),
-        in_specs=[whole(tok), hbm] + [whole(a) for a in (seg, pk, pv, wo, bo, g1, s1, db)] + [hbm, hbm],
+        in_specs=[hbm] * 5 + [whole(a) for a in (seg, pk, pv, bo, g1, s1, db, ub)],
         out_specs=[o[0] for o in outs],
         out_shape=[o[1] for o in outs],
-        scratch_shapes=[pltpu.VMEM((length, width), t) for t in (BF16, BF16, BF16, BF16, F32, F32)] + [
+        scratch_shapes=[pltpu.VMEM((length, width), t) for t in (BF16, BF16, BF16, BF16, F32, F32, BF16)] + [
+            pltpu.VMEM((width, width), BF16),
+            pltpu.VMEM(up_shape, BF16),
             pltpu.VMEM(wqkv.shape, BF16),
             pltpu.VMEM((width, length), BF16),
             pltpu.VMEM((width, pre), BF16),
@@ -542,7 +557,7 @@
             pltpu.VMEM((2, window + pre, 2 * QB), F32),
             pltpu.VMEM((width, length), BF16),
             pltpu.VMEM((length, width), BF16),
-            pltpu.VMEM((3, up.shape[0], part), BF16),
+            pltpu.VMEM((3, up_shape[0], part), BF16),
             pltpu.VMEM((3, part, width), BF16),
             pltpu.VMEM((2, 256, part), F32),
             pltpu.VMEM((2, 256, part), BF16),
@@ -550,13 +565,13 @@
             pltpu.SemaphoreType.DMA((2, pieces)),
             pltpu.SemaphoreType.DMA((2, pieces)),
             pltpu.SemaphoreType.DMA((3, 2, 2)),
-            pltpu.SemaphoreType.DMA((3,)),
+            pltpu.SemaphoreType.DMA((6,)),
             pltpu.SemaphoreType.DMA((chips,)),
             pltpu.SemaphoreType.DMA((6,)),
         ],
         compiler_params=pltpu.CompilerParams(vmem_limit_bytes=VMEM_LIMIT, collective_id=0, has_side_effects=True),
         name="attend_forward",
-    )(tok, wqkv, seg, pk, pv, wo, bo, g1, s1, db, up, down)
+    )(tok, wqkv, wo, up, down, seg, pk, pv, bo, g1, s1, db, ub)
 
 
 def ffn_kernel(res_ref, two_ref, dy_ref, slope_ref, up_hbm, down_hbm, up_own, down_own, wo_ref, g1_ref, g2_ref, s2_ref,
@@ -846,7 +861,8 @@
     def col(a):
         return pl.BlockSpec((a.shape[0], PAIR), lambda i: (0, i))
 
-    outs = [kept((length, width), BF16)] + [kept((pre, width), F32)] * 2
+    vmem = pl.BlockSpec(memory_space=pltpu.VMEM)
+    outs = [(vmem, jax.ShapeDtypeStruct((length, width), BF16))] + [(vmem, jax.ShapeDtypeStruct((pre, width), F32))] * 2
     count_q = counts[0] * counts[1] // 8
     piece = (2 * pre // 8, width)
     return pl.pallas_call(
@@ -872,7 +888,7 @@
             pltpu.VMEM((count_q,) + piece, BF16),
             pltpu.VMEM((8,) + piece, BF16),
         ] + [pltpu.SemaphoreType.DMA((n,)) for n in (8, 8, count_q, count_q, 8, 8, 2)],
-        compiler_params=pltpu.CompilerParams(vmem_limit_bytes=VMEM_LIMIT, collective_id=1, has_side_effects=True),
+        compiler_params=pltpu.CompilerParams(vmem_limit_bytes=BACKWARD_LIMIT, collective_id=1, has_side_effects=True),
         name="attend_backward",
     )(p, q, k, v, mix, do, pk, pv, wqkv, gone)
 
@@ -880,12 +896,11 @@
 def on_device(counts, tokens, segment_ids, qkv_weight, prefix_keys, prefix_values, out_weight, out_bias, norm1_gain,
               norm1_shift, up_weight, up_bias, down_weight, down_bias, norm2_gain, norm2_shift, out_grad):
     row = lambda a: a.reshape(1, -1)
-    up_part = jnp.concatenate([up_weight, jnp.broadcast_to(row(up_bias), (BIAS_ROWS, up_bias.shape[0]))], axis=0)
     q, k, v, mix, probs, res, two, up_all, down_all, slope = attend_forward(
-        tokens[0], qkv_weight, segment_ids, prefix_keys, prefix_values, out_weight, row(out_bias), row(norm1_gain),
-        row(norm1_shift), row(down_bias), up_part, down_weight, counts[1])
+        tokens[0], qkv_weight, out_weight, up_weight, down_weight, segment_ids, prefix_keys, prefix_values, row(out_bias),
+        row(norm1_gain), row(norm1_shift), row(down_bias), row(up_bias), counts[1])
     out, grad_one, grad_mixed = feed_forward_backward(
-        res, two, out_grad[0], slope, up_all, down_all, up_part, down_weight, out_weight, row(norm1_gain), row(norm2_gain),
+        res, two, out_grad[0], slope, up_all, down_all, up_weight, down_weight, out_weight, row(norm1_gain), row(norm2_gain),
         row(norm2_shift))
     grad_tokens, total_k, total_v = attend_backward(
         probs, q, k, v, mix, grad_mixed, prefix_keys, prefix_values, qkv_weight, grad_one, counts)

time: 176 us -> 171 us (0.972)
  Pallas kernels: 168 us -> 165 us
  other arithmetic: 1.88 us -> 0 us
    pallas_call x1, Pallas kernels: 92.4 us -> 89.6 us  [attend_forward(): pl.pallas_call(functools.partial(forward_kernel, count_b), grid=(blocks,)...]
    concatenate x1 -> x0, other arithmetic: 1.88 us -> none  [on_device(): jnp.concatenate([up_weight, jnp.broadcast_to(row(up_bias), (BIAS_ROWS, up...]
where the time goes in v5:
time: 171 us
  Pallas kernels  165 us (96%)
  local copies, waits for them, and re-layouts  5.77 us (3%)
    pallas_call x1, Pallas kernels, attend_forward(): pl.pallas_call(functools.partial(forward_kernel, count_b), grid=(blocks,)...  89.6 us
    pallas_call x1, Pallas kernels, attend_backward(): pl.pallas_call(functools.partial(backward_kernel, counts), grid=(pairs,),...  40.4 us
    pallas_call x1, Pallas kernels, feed_forward_backward(): pl.pallas_call(ffn_kernel, grid=(rows // tb,), in_specs=[block] * 3 + [pl...  34.6 us
    unnamed x7, local copies, waits for them, and re-layouts  4.55 us

profile of v5, /device:TPU:0, one launch (start us, length us, event | category | flops | bytes accessed | tf_op | source)
XLA Modules:
  0.0 171.0 jit_solution(10793559210050594411)
XLA Ops:
  0.6 1.2 reshape.34.ub_ref
  1.9 89.6 %attend_forward.1 = (bf16[1024,1024]{1,0:T(8,128)(2,1)}, bf16[1024,1024]{1,0:T(8,128)(2,1)}, bf16[1024,1024]{1,0:T(8,128)(2,1)}, bf16[1024,1024]{1,0:T(8,128)(2,...) custom-call(bf16[1024,1024]{1,0:T(8,128)(2,1)} %bitcast.12, ...), custom_call_target="tpu_custom_call" | custom-call | tf_op jit(solution)/shard_map/attend_forward/pallas_call | solution.py:543
  91.4 34.6 %feed_forward_backward.1 = (bf16[1024,1024]{1,0:T(8,128)(2,1)}, f32[1024,1024]{1,0:T(8,128)}, bf16[1024,1024]{1,0:T(8,128)(2,1)}) custom-call(f32[1024,1024]{1,0:T(8,128)} %get-tuple-element.20.res_ref, f32[1024,1024]{1,0:T(8,128)} %get-tuple-element.21.two_ref, bf16[1024,1024]{1,0:T(8,128)(2,1)} %bitcast.10, ...), custom_call_target="tpu_custom_call" | custom-call | tf_op jit(solution)/shard_map/feed_forward_backward/pallas_call | solution.py:651
  126.0 40.4 %attend_backward.1 = (bf16[1024,1024]{1,0:T(8,128)(2,1)}, f32[64,1024]{1,0:T(8,128)}, f32[64,1024]{1,0:T(8,128)}) custom-call(bf16[8,8,448,256]{3,2,1,0:T(8,128)(2,1)} %get-tuple-element.26.p_ref, bf16[1024,1024]{1,0:T(8,128)(2,1)} %get-tuple-element.27.q_ref, bf16[1024,1024]{1,0:T(8,128)(2,1)} %get-tuple-element.28.k_ref, ...), custom_call_target="tpu_custom_call" | custom-call | tf_op jit(solution)/shard_map/attend_backward/pallas_call | solution.py:868
  166.5 0.0 copy-start.1
  166.5 0.0 copy-start
  166.5 3.1 %copy.23 = bf16[1,1024,1024]{2,1,0:T(8,128)(2,1)} copy(bf16[1,1024,1024]{2,1,0:T(8,128)(2,1)} %bitcast.11) | data formatting | bytes 4194304
  169.6 0.0 copy-done.1
  169.6 0.7 copy.24
  170.3 0.0 copy-done
  170.3 0.7 copy.25
Async XLA Ops:
  166.5 3.2 %copy-start.1 = (f32[64,1024]{1,0:T(8,128)S(1)}, f32[64,1024]{1,0:T(8,128)}, u32[]{:S(2)}) copy-start(f32[64,1024]{1,0:T(8,128)} %get-tuple-element.42) | copy-start | bytes 786436
  166.5 3.9 %copy-start = (f32[64,1024]{1,0:T(8,128)S(1)}, f32[64,1024]{1,0:T(8,128)}, u32[]{:S(2)}) copy-start(f32[64,1024]{1,0:T(8,128)} %get-tuple-element.43) | copy-start | bytes 786436

commit v6 on v5

--- a/solution.py
+++ b/solution.py
@@ -297,13 +297,13 @@
 
 
 def forward_kernel(count_b, tok_hbm, wqkv_hbm, wo_hbm, up_hbm, down_in, seg_ref, pk_ref, pv_ref, bo_ref, g1_ref, s1_ref, db_ref, ub_ref,
-                   q_hbm, k_hbm, v_hbm, mix_hbm, p_out, res_hbm, two_hbm, up_all, down_all, slope_out,
-                   q_out, k_out, v_out, mix_out, res_out, two, tok_ref, wo_ref, up_in, wqkv_ref, vt, pvt, segc, bias, sbuf, mixt, low, up_v, down_v, pre, hid, slope, send, recv, wsem, qsem, osem, xsem):
+                   q_hbm, k_hbm, v_hbm, mix_hbm, p_out, hat_hbm, two_hbm, up_all, down_all, slope_out, inv_hbm,
+                   q_out, k_out, v_out, mix_out, hat_v, two, inv_v, tok_ref, wo_ref, up_in, wqkv_ref, vt, pvt, segc, bias, sbuf, mixt, low, up_v, down_v, pre, hid, slope, send, recv, wsem, qsem, osem, xsem):
     qb = pl.program_id(0)
 
     def copy_out(n):
-        src = (q_out, k_out, v_out, mix_out, res_out, two)[n]
-        return pltpu.make_async_copy(src, (q_hbm, k_hbm, v_hbm, mix_hbm, res_hbm, two_hbm)[n], xsem.at[n])
+        src = (q_out, k_out, v_out, mix_out, hat_v, two, inv_v)[n]
+        return pltpu.make_async_copy(src, (q_hbm, k_hbm, v_hbm, mix_hbm, hat_hbm, two_hbm, inv_hbm)[n], xsem.at[n])
 
     gather = Gather(count_b, (up_in, down_in), (up_all, down_all), (send, recv))
 
@@ -410,11 +410,14 @@
         for r in range(length // 256):
             rr = slice(r * 256, (r + 1) * 256)
             res = tok_ref[rr].astype(F32) + dot(mix_out[rr], wo_ref[...]) + bo_ref[...]
-            res_out[rr] = res
-            first = normalize(res)[0] * g1_ref[...] + s1_ref[...]
+            hat, inv = normalize(res)
+            hat_v[rr] = hat
+            inv_v[rr] = jnp.broadcast_to(inv, (256, 128))
+            first = hat * g1_ref[...] + s1_ref[...]
             low[rr] = first.astype(BF16)
             two[rr] = first + db_ref[...]
         copy_out(4).start()
+        copy_out(6).start()
         pass_on(9)
 
         chips = LINE * count_b
@@ -519,7 +522,7 @@
             gather.close(t)
         for o in range(chips):
             keep(o).wait()
-        for n in range(6):
+        for n in range(7):
             copy_out(n).wait()
 
 
@@ -537,7 +540,7 @@
     up_shape = (width + BIAS_ROWS, up.shape[1])
     outs += [(hbm, jax.ShapeDtypeStruct((group,) + shape, BF16)) for shape in (up_shape, down.shape)]
     chips, part = group // 2, 2 * down.shape[0]
-    outs += [(hbm, jax.ShapeDtypeStruct((chips, length, part), BF16))]
+    outs += [(hbm, jax.ShapeDtypeStruct((chips, length, part), BF16)), (hbm, jax.ShapeDtypeStruct((length, 128), F32))]
     count_b = group // (2 * LINE)
     pieces = len(gather_keys(count_b))
     return pl.pallas_call(
@@ -546,7 +549,9 @@
         in_specs=[hbm] * 5 + [whole(a) for a in (seg, pk, pv, bo, g1, s1, db, ub)],
         out_specs=[o[0] for o in outs],
         out_shape=[o[1] for o in outs],
-        scratch_shapes=[pltpu.VMEM((length, width), t) for t in (BF16, BF16, BF16, BF16, F32, F32, BF16)] + [
+        scratch_shapes=[pltpu.VMEM((length, width), t) for t in (BF16, BF16, BF16, BF16, F32, F32)] + [
+            pltpu.VMEM((length, 128), F32),
+            pltpu.VMEM((length, width), BF16),
             pltpu.VMEM((width, width), BF16),
             pltpu.VMEM(up_shape, BF16),
             pltpu.VMEM(wqkv.shape, BF16),
@@ -567,14 +572,14 @@
             pltpu.SemaphoreType.DMA((3, 2, 2)),
             pltpu.SemaphoreType.DMA((6,)),
             pltpu.SemaphoreType.DMA((chips,)),
-            pltpu.SemaphoreType.DMA((6,)),
+            pltpu.SemaphoreType.DMA((7,)),
         ],
         compiler_params=pltpu.CompilerParams(vmem_limit_bytes=VMEM_LIMIT, collective_id=0, has_side_effects=True),
         name="attend_forward",
     )(tok, wqkv, wo, up, down, seg, pk, pv, bo, g1, s1, db, ub)
 
 
-def ffn_kernel(res_ref, two_ref, dy_ref, slope_ref, up_hbm, down_hbm, up_own, down_own, wo_ref, g1_ref, g2_ref, s2_ref,
+def ffn_kernel(hat_ref, inv_ref, two_ref, dy_ref, slope_ref, up_hbm, down_hbm, up_own, down_own, wo_ref, g1_ref, g2_ref, s2_ref,
                out_ref, gone_ref, gmix_ref, up, down, hid, low, acc, sems):
     step = pl.program_id(0)
     width = up.shape[0]
@@ -590,16 +595,23 @@
 
     @pl.when(step == 0)
     def _():
-        for t in (1, 0):
-            for d in range(parts):
-
-                @pl.when(me == d)
-                def _():
-                    fetch(d, t, True).start()
-
-                @pl.when(me != d)
-                def _():
-                    fetch(d, t, False).start()
+        for h in range(2):
+            for t in (1, 0):
+                for d in range(h * parts // 2, (h + 1) * parts // 2):
+
+                    @pl.when(me == d)
+                    def _():
+                        fetch(d, t, True).start()
+
+                    @pl.when(me != d)
+                    def _():
+                        fetch(d, t, False).start()
+
+    def await_half(t, h):
+        @pl.when(step == 0)
+        def _():
+            for d in range(h * parts // 2, (h + 1) * parts // 2):
+                fetch(d, t, False).wait()
 
     hat2, inv2 = normalize(two_ref[...])
     out_ref[...] = (hat2 * g2_ref[...] + s2_ref[...]).astype(BF16)
@@ -607,11 +619,6 @@
     acc[...] = grad_two
     low[...] = grad_two.astype(BF16)
 
-    @pl.when(step == 0)
-    def _():
-        for d in range(parts):
-            fetch(d, 1, False).wait()
-
     def cols_of(j):
         return slice(j * chunk, (j + 1) * chunk)
 
@@ -622,27 +629,24 @@
     def back_up(j):
         acc[...] += dot_t(hid[j % 2], up[:, cols_of(j)])
 
+    await_half(1, 0)
     for j in range(count + 1):
+        if j == count // 2:
+            await_half(1, 1)
         if j < count:
             back_down(j)
-        if j == 1:
-
-            @pl.when(step == 0)
-            def _():
-                for d in range(parts):
-                    fetch(d, 0, False).wait()
-
+        if j in (1, count // 2 + 1):
+            await_half(0, j // (count // 2 + 1))
         if j >= 1:
             back_up(j - 1)
 
-    hat, inv1 = normalize(res_ref[...])
-    grad_one = norm_back(acc[...], hat, inv1, g1_ref[...])
+    grad_one = norm_back(acc[...], hat_ref[...], inv_ref[:, 0:1], g1_ref[...])
     gone_ref[...] = grad_one
     gmix_ref[...] = dot_t(grad_one.astype(BF16), wo_ref[...]).astype(BF16)
 
 
-def feed_forward_backward(res, two, dy, slope, up, down, up_own, down_own, wo, g1, g2, s2, tb=256):
-    rows, width = res.shape
+def feed_forward_backward(hat, inv, two, dy, slope, up, down, up_own, down_own, wo, g1, g2, s2, tb=256):
+    rows, width = hat.shape
     parts, ffl, _ = down.shape
     ff = parts * ffl
     chips, _, part = slope.shape
@@ -651,7 +655,7 @@
     return pl.pallas_call(
         ffn_kernel,
         grid=(rows // tb,),
-        in_specs=[block] * 3 + [pl.BlockSpec((chips, tb, part), lambda i: (0, i, 0))] + [hbm] * 4
+        in_specs=[block, pl.BlockSpec((tb, 128), lambda i: (i, 0))] + [block] * 2 + [pl.BlockSpec((chips, tb, part), lambda i: (0, i, 0))] + [hbm] * 4
         + [whole(a) for a in (wo, g1, g2, s2)],
         out_specs=[block] * 3,
         out_shape=[jax.ShapeDtypeStruct((rows, width), t) for t in (BF16, F32, BF16)],
@@ -665,7 +669,7 @@
         ],
         compiler_params=pltpu.CompilerParams(vmem_limit_bytes=VMEM_LIMIT),
         name="feed_forward_backward",
-    )(res, two, dy, slope, up, down, up_own, down_own, wo, g1, g2, s2)
+    )(hat, inv, two, dy, slope, up, down, up_own, down_own, wo, g1, g2, s2)
 
 
 class Total:
@@ -710,12 +714,13 @@
     def peers(self, phase):
         return range(1, self.count_q if phase == 1 else 8)
 
+    def partners(self):
+        return [self.near(j) for j in self.peers(0)] + [self.far(i) for i in self.peers(1)]
+
     def greet(self):
         barrier = pltpu.get_barrier_semaphore()
-        partners = [self.near(j) for j in self.peers(0)] + [self.far(i) for i in self.peers(1)]
-        for device in partners:
+        for device in self.partners():
             pl.semaphore_signal(barrier, inc=1, device_id=device, device_id_type=pl.DeviceIdType.MESH)
-        pl.semaphore_wait(barrier, len(partners))
 
     def start(self, phase):
         for j in self.peers(phase):
@@ -726,7 +731,7 @@
             self.copy(phase, j, True).wait_recv()
 
     def first(self):
-        self.greet()
+        pl.semaphore_wait(pltpu.get_barrier_semaphore(), len(self.partners()))
         self.start(0)
 
     def second(self):
@@ -758,8 +763,11 @@
     pair = pl.program_id(0)
     loads = [pltpu.make_async_copy(w_hbm, w_ref, late.at[0]), pltpu.make_async_copy(gone_hbm, gone_ref, late.at[1])]
 
+    total = Total(*counts, low, slots, parts, result, ((send0, recv0), (send1, recv1), (send2, recv2)))
+
     @pl.when(pair == 0)
     def _():
+        total.greet()
         for copy in loads:
             copy.start()
 
@@ -822,7 +830,6 @@
 
     @pl.when(pair == pl.num_programs(0) - 1)
     def _():
-        total = Total(*counts, low, slots, parts, result, ((send0, recv0), (send1, recv1), (send2, recv2)))
         total.first()
 
         def query_grads(i, carry):
@@ -893,17 +900,36 @@
     )(p, q, k, v, mix, do, pk, pv, wqkv, gone)
 
 
+def hand_over_kernel(*refs):
+    n = len(refs) // 2
+    for src, dst in zip(refs[:n], refs[n:]):
+        dst[...] = src[...]
+
+
+def hand_over(*arrays):
+    steps = 4
+    specs = [pl.BlockSpec((a.shape[0] // steps, a.shape[1]), lambda i: (i, 0)) for a in arrays]
+    return pl.pallas_call(
+        hand_over_kernel,
+        grid=(steps,),
+        in_specs=specs,
+        out_specs=specs,
+        out_shape=[jax.ShapeDtypeStruct(a.shape, a.dtype) for a in arrays],
+        name="hand_over",
+    )(*arrays)
+
+
 def on_device(counts, tokens, segment_ids, qkv_weight, prefix_keys, prefix_values, out_weight, out_bias, norm1_gain,
               norm1_shift, up_weight, up_bias, down_weight, down_bias, norm2_gain, norm2_shift, out_grad):
     row = lambda a: a.reshape(1, -1)
-    q, k, v, mix, probs, res, two, up_all, down_all, slope = attend_forward(
+    q, k, v, mix, probs, hat, two, up_all, down_all, slope, inv = attend_forward(
         tokens[0], qkv_weight, out_weight, up_weight, down_weight, segment_ids, prefix_keys, prefix_values, row(out_bias),
         row(norm1_gain), row(norm1_shift), row(down_bias), row(up_bias), counts[1])
     out, grad_one, grad_mixed = feed_forward_backward(
-        res, two, out_grad[0], slope, up_all, down_all, up_weight, down_weight, out_weight, row(norm1_gain), row(norm2_gain),
+        hat, inv, two, out_grad[0], slope, up_all, down_all, up_weight, down_weight, out_weight, row(norm1_gain), row(norm2_gain),
         row(norm2_shift))
-    grad_tokens, total_k, total_v = attend_backward(
-        probs, q, k, v, mix, grad_mixed, prefix_keys, prefix_values, qkv_weight, grad_one, counts)
+    grad_tokens, total_k, total_v = hand_over(*attend_backward(
+        probs, q, k, v, mix, grad_mixed, prefix_keys, prefix_values, qkv_weight, grad_one, counts))
     return out[None], grad_tokens[None], total_k, total_v
 
 

time: 171 us -> 167 us (0.977)
  local copies, waits for them, and re-layouts: 5.77 us -> 1.22 us
    unnamed x7 -> x0, local copies, waits for them, and re-layouts: 4.55 us -> none
    pallas_call x1 -> x2, Pallas kernels: 34.6 us -> 37.1 us  [the longest x1 33.2 us: feed_forward_backward(): pl.pallas_call(ffn_kernel, grid=(rows // tb,), in_specs=[block, pl.BlockS...]
    pallas_call x1, Pallas kernels: 40.4 us -> 38.5 us  [attend_backward(): pl.pallas_call(functools.partial(backward_kernel, counts), grid=(pairs,),...]
where the time goes in v6:
time: 167 us
  Pallas kernels  165 us (99%)
    pallas_call x1, Pallas kernels, attend_forward(): pl.pallas_call(functools.partial(forward_kernel, count_b), grid=(blocks,)...  89.6 us
    pallas_call x1, Pallas kernels, attend_backward(): pl.pallas_call(functools.partial(backward_kernel, counts), grid=(pairs,),...  38.5 us
    pallas_call x1, Pallas kernels, feed_forward_backward(): pl.pallas_call(ffn_kernel, grid=(rows // tb,), in_specs=[block, pl.BlockS...  33.2 us
    pallas_call x1, Pallas kernels, hand_over(): pl.pallas_call(hand_over_kernel, grid=(steps,), in_specs=specs, out_specs...  3.94 us

profile of v6, /device:TPU:0, one launch (start us, length us, event | category | flops | bytes accessed | tf_op | source)
XLA Modules:
  0.0 167.1 jit_solution(13350455135425170240)
XLA Ops:
  0.6 1.2 reshape.34.ub_ref
  1.9 89.6 %attend_forward.1 = (bf16[1024,1024]{1,0:T(8,128)(2,1)}, bf16[1024,1024]{1,0:T(8,128)(2,1)}, bf16[1024,1024]{1,0:T(8,128)(2,1)}, bf16[1024,1024]{1,0:T(8,128)(2,...) custom-call(bf16[1024,1024]{1,0:T(8,128)(2,1)} %bitcast.11, ...), custom_call_target="tpu_custom_call" | custom-call | tf_op jit(solution)/shard_map/attend_forward/pallas_call | solution.py:546
  91.5 33.2 %feed_forward_backward.1 = (bf16[1024,1024]{1,0:T(8,128)(2,1)}, f32[1024,1024]{1,0:T(8,128)}, bf16[1024,1024]{1,0:T(8,128)(2,1)}) custom-call(f32[1024,1024]{1,0:T(8,128)} %get-tuple-element.24.hat_ref, f32[1024,128]{1,0:T(8,128)} %get-tuple-element.25.inv_ref, f32[1024,1024]{1,0:T(8,128)} %get-tuple-element.26.two_ref, bf16[1024,1024]{1,0:T(8,128)(2,1)} %bitcast.10, ...), custom_call_target="tpu_custom_call" | custom-call | tf_op jit(solution)/shard_map/feed_forward_backward/pallas_call | solution.py:655
  124.6 38.5 %attend_backward.1 = (bf16[1024,1024]{1,0:T(8,128)(2,1)}, f32[64,1024]{1,0:T(8,128)}, f32[64,1024]{1,0:T(8,128)}) custom-call(bf16[8,8,448,256]{3,2,1,0:T(8,128)(2,1)} %get-tuple-element.31.p_ref, bf16[1024,1024]{1,0:T(8,128)(2,1)} %get-tuple-element.32.q_ref, bf16[1024,1024]{1,0:T(8,128)(2,1)} %get-tuple-element.33.k_ref, ...), custom_call_target="tpu_custom_call" | custom-call | tf_op jit(solution)/shard_map/attend_backward/pallas_call | solution.py:875
  163.1 3.9 %hand_over.1 = (bf16[1024,1024]{1,0:T(8,128)(2,1)}, f32[64,1024]{1,0:T(8,128)}, f32[64,1024]{1,0:T(8,128)}) custom-call(bf16[1024,1024]{1,0:T(8,128)(2,1)} %get-tuple-element.38.refs_0_, f32[64,1024]{1,0:T(8,128)} %get-tuple-element.39.refs_1_, f32[64,1024]{1,0:T(8,128)} %get-tuple-element.40.refs_2_), custom_call_target="tpu_custom_call" | custom-call | tf_op jit(solution)/shard_map/hand_over/pallas_call | solution.py:912

commit v7 on v6

--- a/solution.py
+++ b/solution.py
@@ -298,7 +298,7 @@
 
 def forward_kernel(count_b, tok_hbm, wqkv_hbm, wo_hbm, up_hbm, down_in, seg_ref, pk_ref, pv_ref, bo_ref, g1_ref, s1_ref, db_ref, ub_ref,
                    q_hbm, k_hbm, v_hbm, mix_hbm, p_out, hat_hbm, two_hbm, up_all, down_all, slope_out, inv_hbm,
-                   q_out, k_out, v_out, mix_out, hat_v, two, inv_v, tok_ref, wo_ref, up_in, wqkv_ref, vt, pvt, segc, bias, sbuf, mixt, low, up_v, down_v, pre, hid, slope, send, recv, wsem, qsem, osem, xsem):
+                   q_out, k_out, v_out, mix_out, hat_v, two, inv_v, tok_ref, wo_ref, up_in, wqkv_ref, vt, pvt, segc, bias, sbuf, mixt, low, up_v, down_v, pre, hid, slope, send, recv, wsem, qsem, osem, xsem, tsem):
     qb = pl.program_id(0)
 
     def copy_out(n):
@@ -513,17 +513,25 @@
             return carry
 
         lax.fori_loop(1, chips, chip_step, 0)
+        def rows_out(b):
+            return pltpu.make_async_copy(two.at[rows_of(b)], two_hbm.at[rows_of(b)], tsem.at[b])
+
+        for b in range(per - 2):
+            rows_out(b).start()
         act(chips - 1, per - 1)
         down(chips - 1, per - 2)
+        rows_out(per - 2).start()
         down(chips - 1, per - 1)
-        copy_out(5).start()
+        rows_out(per - 1).start()
         keep(chips - 1).start()
         for t in range(2):
             gather.close(t)
         for o in range(chips):
             keep(o).wait()
-        for n in range(7):
+        for n in (0, 1, 2, 3, 4, 6):
             copy_out(n).wait()
+        for b in range(per):
+            rows_out(b).wait()
 
 
 def attend_forward(tok, wqkv, wo, up, down, seg, pk, pv, bo, g1, s1, db, ub, group):
@@ -573,6 +581,7 @@
             pltpu.SemaphoreType.DMA((6,)),
             pltpu.SemaphoreType.DMA((chips,)),
             pltpu.SemaphoreType.DMA((7,)),
+            pltpu.SemaphoreType.DMA((length // 256,)),
         ],
         compiler_params=pltpu.CompilerParams(vmem_limit_bytes=VMEM_LIMIT, collective_id=0, has_side_effects=True),
         name="attend_forward",

time: 167 us -> 167 us (level)
  no operation moved by 1% of the time
where the time goes in v7:
time: 167 us
  Pallas kernels  165 us (99%)
    pallas_call x1, Pallas kernels, attend_forward(): pl.pallas_call(functools.partial(forward_kernel, count_b), grid=(blocks,)...  89.2 us
    pallas_call x1, Pallas kernels, attend_backward(): pl.pallas_call(functools.partial(backward_kernel, counts), grid=(pairs,),...  38.5 us
    pallas_call x1, Pallas kernels, feed_forward_backward(): pl.pallas_call(ffn_kernel, grid=(rows // tb,), in_specs=[block, pl.BlockS...  33.2 us
    pallas_call x1, Pallas kernels, hand_over(): pl.pallas_call(hand_over_kernel, grid=(steps,), in_specs=specs, out_specs...  3.94 us

profile of v7, /device:TPU:0, one launch (start us, length us, event | category | flops | bytes accessed | tf_op | source)
XLA Modules:
  0.0 166.7 jit_solution(16475823811067370731)
XLA Ops:
  0.6 1.2 reshape.34.ub_ref
  1.9 89.2 %attend_forward.1 = (bf16[1024,1024]{1,0:T(8,128)(2,1)}, bf16[1024,1024]{1,0:T(8,128)(2,1)}, bf16[1024,1024]{1,0:T(8,128)(2,1)}, bf16[1024,1024]{1,0:T(8,128)(2,...) custom-call(bf16[1024,1024]{1,0:T(8,128)(2,1)} %bitcast.11, ...), custom_call_target="tpu_custom_call" | custom-call | tf_op jit(solution)/shard_map/attend_forward/pallas_call | solution.py:554
  91.0 33.2 %feed_forward_backward.1 = (bf16[1024,1024]{1,0:T(8,128)(2,1)}, f32[1024,1024]{1,0:T(8,128)}, bf16[1024,1024]{1,0:T(8,128)(2,1)}) custom-call(f32[1024,1024]{1,0:T(8,128)} %get-tuple-element.24.hat_ref, f32[1024,128]{1,0:T(8,128)} %get-tuple-element.25.inv_ref, f32[1024,1024]{1,0:T(8,128)} %get-tuple-element.26.two_ref, bf16[1024,1024]{1,0:T(8,128)(2,1)} %bitcast.10, ...), custom_call_target="tpu_custom_call" | custom-call | tf_op jit(solution)/shard_map/feed_forward_backward/pallas_call | solution.py:664
  124.2 38.5 %attend_backward.1 = (bf16[1024,1024]{1,0:T(8,128)(2,1)}, f32[64,1024]{1,0:T(8,128)}, f32[64,1024]{1,0:T(8,128)}) custom-call(bf16[8,8,448,256]{3,2,1,0:T(8,128)(2,1)} %get-tuple-element.31.p_ref, bf16[1024,1024]{1,0:T(8,128)(2,1)} %get-tuple-element.32.q_ref, bf16[1024,1024]{1,0:T(8,128)(2,1)} %get-tuple-element.33.k_ref, ...), custom_call_target="tpu_custom_call" | custom-call | tf_op jit(solution)/shard_map/attend_backward/pallas_call | solution.py:884
  162.8 3.9 %hand_over.1 = (bf16[1024,1024]{1,0:T(8,128)(2,1)}, f32[64,1024]{1,0:T(8,128)}, f32[64,1024]{1,0:T(8,128)}) custom-call(bf16[1024,1024]{1,0:T(8,128)(2,1)} %get-tuple-element.38.refs_0_, f32[64,1024]{1,0:T(8,128)} %get-tuple-element.39.refs_1_, f32[64,1024]{1,0:T(8,128)} %get-tuple-element.40.refs_2_), custom_call_target="tpu_custom_call" | custom-call | tf_op jit(solution)/shard_map/hand_over/pallas_call | solution.py:921
